TPU v7x, 32 devices: a whole 2x2x4 slice. The times are simulated.
32 devices in a mesh: groups: 2 (over y), seq: 8 (over z, x), tensor: 2 (over core).
Axes of the slice: x: 2, y: 2, z: 4, core: 2. Of those that a mesh axis runs over, the one named last changes fastest.
Arguments:
- strain: float32 [3, 14336], P(None, ('groups', 'seq')), parts along dimension 1, may hold values from -6 to 6
- offsets: int32 [6], P('groups'), parts along dimension 0, may hold values from 0 to 128, as said below
- dilation: int32 [2], replicated, may hold values from 1 to 512, as said below
- input_weight: float32 [3, 512], replicated, may hold values from -3.5 to 3.5
- conv_weight: bfloat16 [2, 1024, 2, 512], P(None, None, None, 'tensor'), may hold values from -0.1875 to 0.1875
- conv_bias: float32 [2, 2, 512], P(None, None, 'tensor'), may hold values from -3 to 3
- out_weight: bfloat16 [2, 512, 512], P(None, 'tensor'), may hold values from -0.25 to 0.25
- cotangent: bfloat16 [14336, 512], P(('groups', 'seq')), parts along dimension 0, may hold values from -6 to 6
Outputs:
- grad_input: float32 [6, 512], P('groups'), parts along dimension 0
- grad_conv: float32 [4, 1024, 2, 512], P('groups', 'seq', None, 'tensor'), parts along dimension 0
- grad_bias: float32 [4, 2, 512], P('groups', None, 'tensor'), parts along dimension 0
- grad_out: float32 [4, 512, 512], P('groups', 'tensor'), parts along dimension 0
There are 2 independent parts, one for each index of `groups`. A program takes and returns all parts, laid end to end along the dimension named above; an argument that names none is the same for every part. Nothing has to cross between parts.
Inputs may be any that keep to these rules, and one draw needn't show every extreme that they name: `offsets`: one detector's delay is exactly 128. Powers of two; exactly one layer's dilation is 2 ** 9.
All inputs are finite; a program needn't handle non-finite values.
Results may differ from a plain program's by a relative error of at most 0.01.
Values may be sent and summed in bfloat16 or wider, within the bound.
No kernel may reach another device: no remote copies, remote signals or barrier semaphores. Data moves between devices by JAX's collectives and lax.ppermute only.
A program may use at most 64 MiB of HBM per device.

v0:
```python
import math

import jax
import jax.numpy as jnp
from jax import lax
from jax.sharding import PartitionSpec as P

DET = 3
RESIDUAL_LAYERS = 2
DILATION_EXPONENT = 9
MAXSHIFT = 128


def passed_along(block, axis, distance):
    devices = range(lax.axis_size(axis))
    route = [(i - distance, i) for i in devices if i - distance in devices]
    return lax.ppermute(block, axis, route)


def contract_rows(left_arg, right_arg):
    return lax.dot_general(
        left_arg, right_arg, (((0,), (0,)), ((), ())), preferred_element_type=jnp.float32
    )


def contract_cols(left_arg, right_arg):
    return lax.dot_general(
        left_arg, right_arg, (((1,), (1,)), ((), ())), preferred_element_type=jnp.float32
    )


def body(strain, offsets, dilation, input_weight, conv_weight, conv_bias, out_weight, cotangent):
    rows_here = strain.shape[1]
    channels = input_weight.shape[1]
    local_width = conv_weight.shape[3]
    lag_extent = 2**DILATION_EXPONENT
    seq_count = lax.axis_size("seq")
    prev_strain = passed_along(strain[:, rows_here - MAXSHIFT :], "seq", 1)
    widened = jnp.concatenate([prev_strain, strain], axis=1)
    signal = jnp.stack(
        [
            lax.dynamic_slice_in_dim(widened[detector], MAXSHIFT - offsets[detector], rows_here, 0)
            for detector in range(DET)
        ]
    )
    hidden = lax.dot_general(
        signal,
        input_weight,
        (((0,), (0,)), ((), ())),
        precision=lax.Precision.HIGHEST,
        preferred_element_type=jnp.float32,
    ).astype(jnp.bfloat16)
    stored = []
    for layer_idx in range(RESIDUAL_LAYERS):
        step_lag = dilation[layer_idx]
        tail_rows = hidden[rows_here - lag_extent :]
        before = passed_along(tail_rows, "seq", 1)
        lengthened_signal = jnp.concatenate([before, hidden], axis=0)
        lagged = lax.dynamic_slice_in_dim(lengthened_signal, lag_extent - step_lag, rows_here, 0)
        joined = jnp.concatenate([lagged, hidden], axis=1)
        weight_now = conv_weight[layer_idx].reshape(2 * channels, 2 * local_width)
        bias_now = conv_bias[layer_idx].reshape(2 * local_width)
        preact = jnp.dot(joined, weight_now, preferred_element_type=jnp.float32) + bias_now
        gate_out = (
            jnp.tanh(preact[:, :local_width]) * jax.nn.sigmoid(preact[:, local_width:])
        ).astype(jnp.bfloat16)
        partial_mix = jnp.dot(gate_out, out_weight[layer_idx], preferred_element_type=jnp.float32)
        mixed_sum = lax.psum(partial_mix.astype(jnp.bfloat16), "tensor").astype(jnp.float32)
        stored.append((joined, preact, gate_out))
        hidden = (hidden.astype(jnp.float32) + mixed_sum).astype(jnp.bfloat16)
    adjoint = cotangent.astype(jnp.float32) * (1.0 / math.sqrt(rows_here * seq_count))
    conv_terms = []
    proj_terms = []
    bias_terms = []
    for layer_idx in reversed(range(RESIDUAL_LAYERS)):
        joined, preact, gate_out = stored[layer_idx]
        step_lag = dilation[layer_idx]
        adjoint_low = adjoint.astype(jnp.bfloat16)
        grad_gated = contract_cols(adjoint_low, out_weight[layer_idx])
        proj_terms.insert(0, contract_rows(gate_out, adjoint_low))
        tanh_part = jnp.tanh(preact[:, :local_width])
        sigm_part = jax.nn.sigmoid(preact[:, local_width:])
        grad_pre = jnp.concatenate(
            [
                grad_gated * sigm_part * (1.0 - tanh_part * tanh_part),
                grad_gated * tanh_part * sigm_part * (1.0 - sigm_part),
            ],
            axis=1,
        )
        bias_terms.insert(0, jnp.sum(grad_pre, axis=0).reshape(2, local_width))
        grad_low = grad_pre.astype(jnp.bfloat16)
        next_rows = passed_along(grad_low[:lag_extent], "seq", -1)
        lengthened_signal = jnp.concatenate([grad_low, next_rows], axis=0)
        leading = lax.dynamic_slice_in_dim(lengthened_signal, step_lag, rows_here, 0)
        weight_now = conv_weight[layer_idx].reshape(2 * channels, 2 * local_width)
        adj_term = contract_cols(grad_low, weight_now[channels:]) + contract_cols(
            leading, weight_now[:channels]
        )
        adjoint = adjoint + lax.psum(adj_term.astype(jnp.bfloat16), "tensor").astype(jnp.float32)
        conv_terms.insert(0, contract_rows(joined, grad_low))
    input_term = lax.dot_general(
        signal,
        adjoint,
        (((1,), (0,)), ((), ())),
        precision=lax.Precision.HIGHEST,
        preferred_element_type=jnp.float32,
    )
    grad_out, grad_bias, grad_input = lax.psum(
        (jnp.stack(proj_terms), jnp.stack(bias_terms), input_term), "seq"
    )
    grad_conv = lax.psum_scatter(jnp.stack(conv_terms), "seq", scatter_dimension=1, tiled=True)
    grad_conv = grad_conv.reshape(RESIDUAL_LAYERS, grad_conv.shape[1], 2, local_width)
    return (grad_input, grad_conv, grad_bias, grad_out)


def solution(mesh):
    in_specs = (
        P(None, ("groups", "seq")),
        P("groups"),
        P(),
        P(),
        P(None, None, None, "tensor"),
        P(None, None, "tensor"),
        P(None, "tensor", None),
        P(("groups", "seq"), None),
    )
    out_specs = (
        P("groups", None),
        P("groups", "seq", None, "tensor"),
        P("groups", None, "tensor"),
        P("groups", "tensor", None),
    )
    return jax.shard_map(body, mesh=mesh, in_specs=in_specs, out_specs=out_specs, check_vma=False)
```

profile of v0, /device:TPU:0, one launch (start us, length us, event | category | flops | bytes accessed | tf_op | source)
XLA Modules:
  0.0 358.6 jit_solution(15018191428976784902)
XLA Ops:
  7.2 0.8 slice.106
  8.1 4.9 %collective-permute-start = (f32[3,128]{1,0:T(4,128)S(1)}, f32[3,128]{1,0:T(4,128)S(1)}, u32[]{:S(2)}, u32[]{:S(2)}) collective-permute-start(f32[3,128]{1,0:T(4,128)S(1)} %slice.106), channel_id=1, source_target_pairs={{0,2},{2,4},{4,6},{6,8},{8,10},{10,12},{12,14},{1,3},{3,5},{5,7},{... | collective-permute-start | bytes 4616 | tf_op jit(solution)/shard_map/ppermute | solution.py:17
  12.9 1.3 fusion.53
  14.3 1.4 fusion.54
  20.6 0.7 constant_dynamic-update-slice_fusion
  21.6 1.7 convolution_convert_fusion.1
  23.2 0.8 slice.140
  24.0 3.5 collective-permute-start.1
  27.5 0.6 slice_bitcast_fusion
  28.1 0.6 copy.13
  28.7 2.2 fusion.51
  31.0 1.2 copy.12
  32.2 6.5 %collective-permute-done.1 = bf16[512,512]{1,0:T(8,128)(2,1)S(1)} collective-permute-done((bf16[512,512]{1,0:T(8,128)(2,1)}, bf16[512,512]{1,0:T(8,128)(2,1)S(1)}, u32[]{:S(2)}, u32[]{:S(2)}) %collective-permute-start.1) | collective-permute-done | bytes 524320 | tf_op jit(solution)/shard_map/ppermute | solution.py:17
  38.7 1.0 fusion.14
  39.7 1.3 convolution_add_fusion.1
  41.1 0.4 multiply_convert_fusion.1
  41.5 1.0 copy-done.23
  42.5 1.4 convolution_convert_fusion
  44.0 21.3 %all-reduce.6.cloned.1.call-done = bf16[896,512]{1,0:T(8,128)(2,1)} async-done(((bf16[896,512]{1,0:T(8,128)(2,1)}), bf16[896,512]{1,0:T(8,128)(2,1)}) %all-reduce.6.cloned.1.call-update) | async-done | bytes 917520 | tf_op jit(solution)/shard_map/psum | solution.py:68
  65.3 1.4 add_convert_fusion.2
  66.7 0.9 slice.143
  67.6 4.5 %collective-permute-start.2 = (bf16[512,512]{1,0:T(8,128)(2,1)}, bf16[512,512]{1,0:T(8,128)(2,1)}, u32[]{:S(2)}, u32[]{:S(2)}) collective-permute-start(bf16[512,512]{1,0:T(8,128)(2,1)} %slice.143), channel_id=1, source_target_pairs={{0,2},{2,4},{4,6},{6,8},{8,10},{10,12},{12,14},{1,3},{3,5},{5,7},{... | collective-permute-start | bytes 1572872 | tf_op jit(solution)/shard_map/ppermute | solution.py:17
  74.7 1.2 copy.14
  75.9 7.3 %collective-permute-done.2 = bf16[512,512]{1,0:T(8,128)(2,1)} collective-permute-done((bf16[512,512]{1,0:T(8,128)(2,1)}, bf16[512,512]{1,0:T(8,128)(2,1)}, u32[]{:S(2)}, u32[]{:S(2)}) %collective-permute-start.2) | collective-permute-done | bytes 524320 | tf_op jit(solution)/shard_map/ppermute | solution.py:17
  83.2 1.7 fusion.13
  84.9 1.3 convolution_add_fusion
  86.6 0.7 subtract_multiply_fusion.3
  87.3 0.6 copy-done.30
  87.9 0.8 slice.146
  89.0 0.3 copy-done.9
  89.2 1.6 collective-permute-start.3
  90.8 2.3 fusion.50
  93.1 0.9 copy.17
  94.1 0.9 copy.16
  95.6 1.8 fusion.55
  97.4 8.2 %collective-permute-done.3 = bf16[512,512]{0,1:T(8,128)(2,1)} collective-permute-done((bf16[512,512]{0,1:T(8,128)(2,1)}, bf16[512,512]{0,1:T(8,128)(2,1)}, u32[]{:S(2)}, u32[]{:S(2)}) %collective-permute-start.3) | collective-permute-done | bytes 524320 | tf_op jit(solution)/shard_map/ppermute | solution.py:17
  105.5 3.4 add_convert_fusion.1
  109.0 20.5 %all-reduce.8.cloned.1.call-done = bf16[896,512]{1,0:T(8,128)(2,1)} async-done(((bf16[896,512]{1,0:T(8,128)(2,1)}), bf16[896,512]{1,0:T(8,128)(2,1)}) %all-reduce.8.cloned.1.call-update) | async-done | bytes 917520 | tf_op jit(solution)/shard_map/psum | solution.py:99
  129.5 2.6 subtract_multiply_fusion.1
  132.1 0.9 copy-done.13
  133.3 0.8 slice.147
  134.1 1.3 collective-permute-start.4
  136.5 1.9 copy.19
  138.4 1.9 copy.18
  140.9 1.8 fusion.56
  142.7 7.7 %collective-permute-done.4 = bf16[512,512]{0,1:T(8,128)(2,1)} collective-permute-done((bf16[512,512]{0,1:T(8,128)(2,1)}, bf16[512,512]{0,1:T(8,128)(2,1)}, u32[]{:S(2)}, u32[]{:S(2)}) %collective-permute-start.4) | collective-permute-done | bytes 524320 | tf_op jit(solution)/shard_map/ppermute | solution.py:17
  150.4 3.5 add_convert_fusion
  154.0 2.8 convolution_bitcast_fusion
  156.9 1.3 convolution_bitcast_fusion.1
  158.2 2.4 pad_maximum_fusion
  160.7 1.1 copy-done.6
  161.8 2.1 convolution_bitcast_fusion.2
  164.0 0.5 convolution_bitcast_fusion.3
  164.5 1.0 pad_maximum_fusion.9
  165.5 0.5 copy-done.8
  166.0 0.3 copy-done.10
  166.5 1.7 fusion.5
  168.2 6.2 %all-reduce.10.cloned.1.call-done = bf16[896,512]{1,0:T(8,128)(2,1)} async-done(((bf16[896,512]{1,0:T(8,128)(2,1)}), bf16[896,512]{1,0:T(8,128)(2,1)}) %all-reduce.10.cloned.1.call-update) | async-done | bytes 917520 | tf_op jit(solution)/shard_map/psum | solution.py:99
  174.4 2.5 fusion
  177.0 38.9 %all-reduce = (f32[3,512]{1,0:T(4,128)}, f32[2,2,256]{2,1,0:T(2,128)}) all-reduce(f32[3,512]{1,0:T(4,128)S(1)} %fusion, f32[2,2,256]{2,1,0:T(2,128)S(1)} %pad_maximum_fusion.13), channel_id=1, replica_groups=mesh['groups'=2,'seq'=8,'tensor'=2] {'seq'}, use_global_device_ids=true, to_apply=%region_3.0 | all-reduce | flops 2560 | bytes 20480 | tf_op jit(solution)/shard_map/psum | solution.py:108
  215.9 52.1 %reduce-scatter.2.cloned.1.call-done = f32[2,128,512]{2,1,0:T(8,128)} async-done(((f32[2,1024,512]{2,1,0:T(8,128)}), f32[2,128,512]{2,1,0:T(8,128)}) %reduce-scatter.2.cloned.1.call-update) | async-done | bytes 524304 | tf_op jit(solution)/shard_map/reduce_scatter | solution.py:111
  267.9 2.2 reshape.35
  270.1 79.7 %all-reduce.12.cloned.1.call-done = f32[2,256,512]{2,1,0:T(8,128)} async-done(((f32[2,256,512]{2,1,0:T(8,128)}), f32[2,256,512]{2,1,0:T(8,128)}) %all-reduce.12.cloned.1.call-update) | async-done | bytes 1048592 | tf_op jit(solution)/shard_map/psum | solution.py:108
  349.9 2.3 copy.25
  (77 shorter events, 1.7 us)
Async XLA Ops:
  7.2 14.4 %copy-start = (f32[3,512]{1,0:T(4,128)S(1)}, f32[3,512]{1,0:T(4,128)}, u32[]{:S(2)}) copy-start(f32[3,512]{1,0:T(4,128)} %param.11) | copy-start | bytes 18436
  7.2 21.5 %copy-start.1 = (bf16[2,1024,2,256]{3,2,1,0:T(2,128)(2,1)S(1)}, bf16[2,1024,2,256]{3,2,1,0:T(2,128)(2,1)}, u32[]{:S(2)}) copy-start(bf16[2,1024,2,256]{3,2,1,0:T(2,128)(2,1)} %param.12) | copy-start | bytes 6291460
  7.2 58.1 %all-reduce.6.cloned.1.call-start = ((), (), s32[]{:S(2)}) async-start(), calls=%async_computation.1 | async-start | bytes 1835008 | tf_op jit(solution)/shard_map/psum | solution.py:68
  8.1 12.6 %collective-permute-start = (f32[3,128]{1,0:T(4,128)S(1)}, f32[3,128]{1,0:T(4,128)S(1)}, u32[]{:S(2)}, u32[]{:S(2)}) collective-permute-start(f32[3,128]{1,0:T(4,128)S(1)} %slice.106), channel_id=1, source_target_pairs={{0,2},{2,4},{4,6},{6,8},{8,10},{10,12},{12,14},{1,3},{3,5},{5,7},{... | collective-permute-start | bytes 4616 | tf_op jit(solution)/shard_map/ppermute | solution.py:17
  20.6 6.9 %copy-start.28 = (f32[2,2,256]{2,1,0:T(2,128)S(1)}, f32[2,2,256]{2,1,0:T(2,128)}, u32[]{:S(2)}) copy-start(f32[2,2,256]{2,1,0:T(2,128)} %param.13) | copy-start | bytes 12292
  21.5 6.6 %copy-start.25 = (f32[1,896]{1,0:T(1,128)}, f32[1,896]{1,0:T(1,128)S(1)}, u32[]{:S(2)}) copy-start(f32[1,896]{1,0:T(1,128)S(1)} %get-tuple-element.27) | copy-start | bytes 10756
  24.0 14.7 %collective-permute-start.1 = (bf16[512,512]{1,0:T(8,128)(2,1)}, bf16[512,512]{1,0:T(8,128)(2,1)S(1)}, u32[]{:S(2)}, u32[]{:S(2)}) collective-permute-start(bf16[512,512]{1,0:T(8,128)(2,1)} %slice.140), channel_id=1, source_target_pairs={{0,2},{2,4},{4,6},{6,8},{8,10},{10,12},{12,14},{1,3},{3,5},{5,7},{... | collective-permute-start | bytes 1572872 | tf_op jit(solution)/shard_map/ppermute | solution.py:17
  31.0 8.8 %copy-start.29 = (f32[1,2,2,128]{3,1,2,0:T(2,128)S(1)}, f32[1,2,2,128]{3,1,2,0:T(2,128)}, u32[]{:S(2)}) copy-start(f32[1,2,2,128]{3,1,2,0:T(2,128)} %copy.13) | copy-start | bytes 6148
  32.2 7.6 %copy-start.18 = (bf16[128,8,2,256]{3,1,2,0:T(8,128)(2,1)S(1)}, bf16[128,8,2,256]{3,1,2,0:T(8,128)(2,1)}, u32[]{:S(2)}) copy-start(bf16[128,8,2,256]{3,1,2,0:T(8,128)(2,1)} %copy.12) | copy-start | bytes 3145732
  39.7 1.3 copy-start.20
  41.1 2.8 copy-start.17
  41.1 1.4 copy-start.23
  43.9 30.8 %copy-start.27 = (f32[1,2,2,128]{3,2,1,0:T(2,128)S(1)}, f32[1,2,2,128]{3,2,1,0:T(2,128)}, u32[]{:S(2)}) copy-start(f32[1,2,2,128]{3,2,1,0:T(2,128)} %get-tuple-element.19) | copy-start | bytes 6148
  43.9 30.8 %copy-start.4 = (bf16[1,1024,2,256]{3,2,1,0:T(2,128)(2,1)S(1)}, bf16[1,1024,2,256]{3,2,1,0:T(2,128)(2,1)}, u32[]{:S(2)}) copy-start(bf16[1,1024,2,256]{3,2,1,0:T(2,128)(2,1)} %get-tuple-element.15) | copy-start | bytes 3145732
  43.9 85.5 %all-reduce.8.cloned.1.call-start = ((), (), s32[]{:S(2)}) async-start(), calls=%async_computation.2 | async-start | bytes 1835008 | tf_op jit(solution)/shard_map/psum | solution.py:99
  66.7 18.2 %copy-start.3 = (bf16[896,512]{1,0:T(8,128)(2,1)}, bf16[896,512]{1,0:T(8,128)(2,1)S(1)}, u32[]{:S(2)}) copy-start(bf16[896,512]{1,0:T(8,128)(2,1)S(1)} %add_convert_fusion.2) | copy-start | bytes 2752516
  67.6 15.6 %collective-permute-start.2 = (bf16[512,512]{1,0:T(8,128)(2,1)}, bf16[512,512]{1,0:T(8,128)(2,1)}, u32[]{:S(2)}, u32[]{:S(2)}) collective-permute-start(bf16[512,512]{1,0:T(8,128)(2,1)} %slice.143), channel_id=1, source_target_pairs={{0,2},{2,4},{4,6},{6,8},{8,10},{10,12},{12,14},{1,3},{3,5},{5,7},{... | collective-permute-start | bytes 1572872 | tf_op jit(solution)/shard_map/ppermute | solution.py:17
  75.9 9.0 %copy-start.19 = (bf16[128,8,2,256]{3,1,2,0:T(8,128)(2,1)S(1)}, bf16[128,8,2,256]{3,1,2,0:T(8,128)(2,1)}, u32[]{:S(2)}) copy-start(bf16[128,8,2,256]{3,1,2,0:T(8,128)(2,1)} %copy.14) | copy-start | bytes 3145732
  84.9 1.4 copy-start.22
  84.9 1.5 copy-start.5
  84.9 1.6 copy-start.24
  86.5 1.3 copy-start.30
  87.8 1.1 copy-start.7
  87.8 1.4 copy-start.9
  87.8 3.0 copy-start.2
  89.2 16.3 %collective-permute-start.3 = (bf16[512,512]{0,1:T(8,128)(2,1)}, bf16[512,512]{0,1:T(8,128)(2,1)}, u32[]{:S(2)}, u32[]{:S(2)}) collective-permute-start(bf16[512,512]{0,1:T(8,128)(2,1)} %slice.146), channel_id=1, source_target_pairs={{2,0},{4,2},{6,4},{8,6},{10,8},{12,10},{14,12},{3,1},{5,3},{7,5},{... | collective-permute-start | bytes 1572872 | tf_op jit(solution)/shard_map/ppermute | solution.py:17
  95.6 10.0 %copy-start.16 = (bf16[64,8,2,256]{3,1,2,0:T(8,128)(2,1)S(1)}, bf16[64,8,2,256]{3,1,2,0:T(8,128)(2,1)}, u32[]{:S(2)}) copy-start(bf16[64,8,2,256]{3,1,2,0:T(8,128)(2,1)} %copy.17) | copy-start | bytes 1572868
  108.9 65.5 %all-reduce.10.cloned.1.call-start = ((), (), s32[]{:S(2)}) async-start(), calls=%async_computation.3 | async-start | bytes 1835008 | tf_op jit(solution)/shard_map/psum | solution.py:99
  132.1 0.9 copy-start.13
  132.1 1.2 copy-start.14
  134.1 16.3 %collective-permute-start.4 = (bf16[512,512]{0,1:T(8,128)(2,1)}, bf16[512,512]{0,1:T(8,128)(2,1)}, u32[]{:S(2)}, u32[]{:S(2)}) collective-permute-start(bf16[512,512]{0,1:T(8,128)(2,1)} %slice.147), channel_id=1, source_target_pairs={{2,0},{4,2},{6,4},{8,6},{10,8},{12,10},{14,12},{3,1},{5,3},{7,5},{... | collective-permute-start | bytes 1572872 | tf_op jit(solution)/shard_map/ppermute | solution.py:17
  140.9 9.5 %copy-start.15 = (bf16[64,8,2,256]{3,1,2,0:T(8,128)(2,1)S(1)}, bf16[64,8,2,256]{3,1,2,0:T(8,128)(2,1)}, u32[]{:S(2)}) copy-start(bf16[64,8,2,256]{3,1,2,0:T(8,128)(2,1)} %copy.19) | copy-start | bytes 1572868
  154.0 114.0 %reduce-scatter.2.cloned.1.call-start = ((), (), s32[]{:S(2)}) async-start(), calls=%async_computation.4 | async-start | bytes 4718592 | tf_op jit(solution)/shard_map/reduce_scatter | solution.py:111
  154.0 2.9 copy-start.21
  160.6 1.2 copy-start.6
  160.6 3.3 copy-start.11
  160.6 189.2 %all-reduce.12.cloned.1.call-start = ((), (), s32[]{:S(2)}) async-start(), calls=%async_computation.5 | async-start | bytes 2097152 | tf_op jit(solution)/shard_map/psum | solution.py:108
  164.5 1.6 copy-start.8
  164.5 1.8 copy-start.10
  166.3 8.1 %copy-start.26 = (f32[1,896]{1,0:T(1,128)S(1)}, f32[1,896]{1,0:T(1,128)}, u32[]{:S(2)}) copy-start(f32[1,896]{1,0:T(1,128)} %copy-done.25) | copy-start | bytes 10756
  166.5 8.0 %copy-start.12 = (bf16[896,512]{1,0:T(8,128)(2,1)S(1)}, bf16[896,512]{1,0:T(8,128)(2,1)}, u32[]{:S(2)}) copy-start(bf16[896,512]{1,0:T(8,128)(2,1)} %all-reduce.8.cloned.1.call-done) | copy-start | bytes 2752516
Sparse Core Ops, SparseCore 0:
  44.0 21.2 all-reduce.5
  109.1 20.3 all-reduce.7
  154.1 20.3 all-reduce.9
  177.9 89.9 reduce-scatter.1
  271.9 77.9 all-reduce.11
where the time goes:
time: 360 us; the launch traced here: 359 us
  waiting for transfers between devices  210 us (58%)
  blocking collectives  38.9 us (11%)
  local copies, waits for them, and re-layouts  31.5 us (9%)
  matrix products  28.6 us (8%)
  between operations  24 us (7%)
  starting transfers between devices  15.9 us (4%)
  other arithmetic  10 us (3%)
    psum x1, waiting for transfers between devices, body(): lax.psum((jnp.stack(proj_terms), jnp.stack(bias_terms), input_term), 'seq')  79.7 us
    reduce_scatter x1, waiting for transfers between devices, body(): lax.psum_scatter(jnp.stack(conv_terms), 'seq', scatter_dimension=1, tiled...  52.1 us
    psum x1, blocking collectives, body(): lax.psum((jnp.stack(proj_terms), jnp.stack(bias_terms), input_term), 'seq')  38.9 us
    ppermute x5, waiting for transfers between devices, passed_along(): return lax.ppermute(block, axis, route)  29.7 us
    psum x2, waiting for transfers between devices, body(): lax.psum(adj_term.astype(jnp.bfloat16), 'tensor').astype(jnp.float32)  26.7 us
    psum x1, waiting for transfers between devices, body(): lax.psum(partial_mix.astype(jnp.bfloat16), 'tensor').astype(jnp.float32)  21.3 us
    unnamed x73, local copies, waits for them, and re-layouts  17 us
    ppermute x5, starting transfers between devices, passed_along(): return lax.ppermute(block, axis, route)  15.7 us
  transfers between devices with their start and end apart: 10, of which 9 were waited for; matrix products, arithmetic and copies ran while one was open for 10% of the time, Pallas kernels for 0%

commit v1 on v0

v1 whole, which is shorter than its diff:
```python
import math

import jax
import jax.numpy as jnp
from jax import lax
from jax.sharding import PartitionSpec as P

DET = 3
DILATION_EXPONENT = 9
MAXSHIFT = 128
LAG = 2**DILATION_EXPONENT
F32 = jnp.float32
BF16 = jnp.bfloat16


def dot(a, b, dims):
    return lax.dot_general(a, b, (dims, ((), ())), preferred_element_type=F32)


def top(x):
    return lax.reduce_precision(x, 8, 7)


def parts(x):
    hi = top(x)
    return hi.astype(BF16), top(x - hi).astype(BF16)


def swap(x):
    return lax.ppermute(x, "tensor", [(0, 1), (1, 0)])


def gates(pre, width):
    return jnp.tanh(pre[:, :width]), jax.nn.sigmoid(pre[:, width:])


def slopes(gg, th, sg):
    return jnp.concatenate([gg * sg * (1.0 - th * th), gg * th * sg * (1.0 - sg)], axis=1)


def scatter_sum(x, n):
    blocks = x.astype(BF16).reshape(n, x.shape[0] // n, x.shape[1])
    got = lax.all_to_all(blocks, "seq", 0, 0, tiled=True)
    return jnp.sum(got.astype(F32), axis=0)


def gather(x, n):
    got = lax.all_to_all(jnp.broadcast_to(x[None], (n,) + x.shape), "seq", 0, 0, tiled=True)
    return got


def body(strain, offsets, dilation, input_weight, conv_weight, conv_bias, out_weight, cotangent):
    rows = strain.shape[1]
    channels = input_weight.shape[1]
    width = conv_weight.shape[3]
    n = lax.axis_size("seq")
    me = lax.axis_index("seq")
    ext = LAG + rows
    scale = 1.0 / math.sqrt(rows * n)
    inside = jnp.where(me == 0, 0.0, 1.0)
    keep = jnp.where(lax.broadcasted_iota(jnp.int32, (ext, 1), 0) < LAG, inside, 1.0)

    prev = lax.ppermute(strain, "seq", [(i, i + 1) for i in range(n - 1)])
    spare = 2 * LAG + MAXSHIFT - rows
    line = jnp.concatenate([jnp.zeros((DET, spare), F32), prev, strain], axis=1)
    starts = [LAG + MAXSHIFT - offsets[k] for k in range(DET)]
    sig = jnp.stack(
        [lax.dynamic_slice_in_dim(line[k], starts[k] - dilation[0], ext, 0) for k in range(DET)]
        + [lax.dynamic_slice_in_dim(line[k], starts[k], ext, 0) for k in range(DET)]
    )
    s_hi, s_lo = parts(sig)
    s3 = jnp.concatenate([s_hi, s_lo, s_hi], axis=0)

    w0 = conv_weight[0].reshape(2 * channels, 2 * width)
    w1 = conv_weight[1].reshape(2 * channels, 2 * width)
    b0 = conv_bias[0].reshape(2 * width)
    b1 = conv_bias[1].reshape(2 * width)
    i_hi, i_lo = parts(input_weight)
    i2 = jnp.concatenate([i_hi, i_lo], axis=0)
    a_lag = dot(i2, w0[:channels], ((1,), (0,)))
    a_cur = dot(i2, w0[channels:], ((1,), (0,)))
    a0 = jnp.concatenate([a_lag[:DET] + a_lag[DET:], a_cur[:DET] + a_cur[DET:]], axis=0)
    a_hi, a_lo = parts(a0)
    a3 = jnp.concatenate([a_hi, a_hi, a_lo], axis=0)

    pre0 = dot(s3, a3, ((0,), (0,))) + b0
    th0, sg0 = gates(pre0, width)
    gate0 = (th0 * sg0).astype(BF16)
    mine = dot(gate0, out_weight[0], ((1,), (0,))).astype(BF16)
    other = swap(mine)
    c3 = jnp.concatenate([s_hi[DET:], s_lo[DET:], s_hi[DET:]], axis=0)
    h0 = dot(c3, jnp.concatenate([i_hi, i_hi, i_lo], axis=0), ((0,), (0,)))
    h1 = ((h0 + mine.astype(F32) + other.astype(F32)) * keep).astype(BF16)

    lag1 = lax.dynamic_slice_in_dim(h1, LAG - dilation[1], rows, 0)
    cur1 = h1[LAG:]
    pre1 = dot(lag1, w1[:channels], ((1,), (0,))) + dot(cur1, w1[channels:], ((1,), (0,))) + b1
    th1, sg1 = gates(pre1, width)
    gate1 = (th1 * sg1).astype(BF16)
    gg1 = dot(cotangent, out_weight[1], ((1,), (1,))) * scale
    gp1 = slopes(gg1, th1, sg1)
    gl1 = gp1.astype(BF16)
    c_cur = dot(gl1, w1[channels:], ((1,), (1,)))
    c_lag = dot(gl1, w1[:channels], ((1,), (1,)))
    base = jnp.concatenate([jnp.zeros((LAG, channels), F32), c_cur], axis=0)
    moved = lax.dynamic_slice_in_dim(
        jnp.concatenate(
            [jnp.zeros((LAG, channels), F32), c_lag, jnp.zeros((LAG, channels), F32)], axis=0
        ),
        dilation[1],
        ext,
        0,
    )
    part = (base + moved).astype(BF16)
    apart = swap(part)

    dw_lag = dot(lag1, gl1, ((0,), (0,)))
    dw_cur = dot(cur1, gl1, ((0,), (0,)))
    dw1 = scatter_sum(jnp.concatenate([dw_lag, dw_cur], axis=0), n)
    do1 = scatter_sum(dot(gate1, cotangent, ((0,), (0,))) * scale, n)

    cot_ext = jnp.concatenate([jnp.zeros((LAG, channels), BF16), cotangent], axis=0)
    adj = part.astype(F32) + apart.astype(F32) + cot_ext.astype(F32) * scale
    adj = (adj * keep).astype(BF16)
    gg0 = dot(adj, out_weight[0], ((1,), (1,)))
    gp0 = slopes(gg0, th0, sg0)
    gl0 = gp0.astype(BF16)
    do0 = scatter_sum(dot(gate0, adj, ((0,), (0,))), n)
    s2 = jnp.concatenate([s_hi, s_lo], axis=0)
    r2 = dot(s2, gl0, ((1,), (0,)))
    r = r2[: 2 * DET] + r2[2 * DET :]
    g2 = dot(jnp.concatenate([s_hi[DET:], s_lo[DET:]], axis=0), adj, ((1,), (0,)))
    first = jnp.where(lax.axis_index("tensor") == 0, 1.0, 0.0)
    g = (g2[:DET] + g2[DET:]) * first
    r_hi, r_lo = parts(r)
    back = dot(jnp.concatenate([r_hi[:DET], r_lo[:DET]], axis=0), w0[:channels], ((1,), (1,)))
    back += dot(jnp.concatenate([r_hi[DET:], r_lo[DET:]], axis=0), w0[channels:], ((1,), (1,)))
    g = g + back[:DET] + back[DET:]
    bias = jnp.stack([jnp.sum(gp0, axis=0), jnp.sum(gp1, axis=0)])
    small = gather(jnp.concatenate([r, g, bias], axis=0), n)
    small = jnp.sum(small, axis=0)
    r, g, bias = small[: 2 * DET], small[2 * DET : 3 * DET], small[3 * DET :]
    grad_input = g + swap(g)
    grad_bias = bias.reshape(2, 2, width)
    block = 2 * channels // n
    mine_iw = lax.dynamic_slice_in_dim(input_weight, (me * block) % channels, block, 1)
    mine_r = jnp.where(me * block < channels, r[:DET], r[DET:])
    dw0 = sum(mine_iw[k][:, None] * mine_r[k][None, :] for k in range(DET))
    grad_conv = jnp.stack([dw0, dw1]).reshape(2, block, 2, width)
    do = gather(jnp.stack([do0, do1]).astype(BF16), n).astype(F32)
    grad_out = jnp.moveaxis(do, 0, 1).reshape(2, width, channels)
    return (grad_input, grad_conv, grad_bias, grad_out)


def solution(mesh):
    in_specs = (
        P(None, ("groups", "seq")),
        P("groups"),
        P(),
        P(),
        P(None, None, None, "tensor"),
        P(None, None, "tensor"),
        P(None, "tensor", None),
        P(("groups", "seq"), None),
    )
    out_specs = (
        P("groups", None),
        P("groups", "seq", None, "tensor"),
        P("groups", None, "tensor"),
        P("groups", "tensor", None),
    )
    return jax.shard_map(body, mesh=mesh, in_specs=in_specs, out_specs=out_specs, check_vma=False)
```

time: 360 us -> 137 us (0.38)
  waiting for transfers between devices: 210 us -> 46.5 us
  blocking collectives: 38.9 us -> 0 us
  between operations: 24 us -> 10.1 us
  local copies, waits for them, and re-layouts: 31.5 us -> 19.1 us
  starting transfers between devices: 15.9 us -> 26.3 us
  matrix products: 28.6 us -> 18.4 us
  other arithmetic: 10 us -> 15.5 us
    psum x4 -> x0, waiting for transfers between devices: 128 us -> none  [the longest x1 79.7 us: body(): lax.psum((jnp.stack(proj_terms), jnp.stack(bias_terms), input_term), 'seq')]
    reduce_scatter x1 -> x0, waiting for transfers between devices: 52.1 us -> none  [body(): lax.psum_scatter(jnp.stack(conv_terms), 'seq', scatter_dimension=1, tiled...]
    all_to_all x0 -> x5, waiting for transfers between devices: none -> 46.5 us  [the longest x3 29.3 us: scatter_sum(): got = lax.all_to_all(blocks, 'seq', 0, 0, tiled=True)]
    psum x1 -> x0, blocking collectives: 38.9 us -> none  [body(): lax.psum((jnp.stack(proj_terms), jnp.stack(bias_terms), input_term), 'seq')]
    ppermute x5 -> x4, waiting for transfers between devices: 29.7 us -> 0.01 us  [the longest x3 0.01 us: swap(): return lax.ppermute(x, 'tensor', [(0, 1), (1, 0)])]
    all_to_all x0 -> x5, starting transfers between devices: none -> 20.8 us  [the longest x3 12 us: scatter_sum(): got = lax.all_to_all(blocks, 'seq', 0, 0, tiled=True)]
    dot_general x15 -> x19, matrix products: 28.6 us -> 18.4 us  [dot(): return lax.dot_general(a, b, (dims, ((), ())), preferred_element_type=F32)]
    ppermute x5 -> x4, starting transfers between devices: 15.7 us -> 5.47 us  [the longest x1 4.87 us: body(): prev = lax.ppermute(strain, 'seq', [(i, i + 1) for i in range(n - 1)])]
  transfers between devices with their start and end apart: 10 -> 9, of which waited for: 9 -> 5; matrix products, arithmetic and copies ran while one was open for 10% -> 24% of each run, Pallas kernels for 0% -> 0%
where the time goes in v1:
time: 137 us; the launch traced here: 136 us
  waiting for transfers between devices  46.5 us (34%)
  starting transfers between devices  26.3 us (19%)
  local copies, waits for them, and re-layouts  19.1 us (14%)
  matrix products  18.4 us (13%)
  other arithmetic  15.5 us (11%)
  between operations  10.1 us (7%)
    all_to_all x3, waiting for transfers between devices, scatter_sum(): got = lax.all_to_all(blocks, 'seq', 0, 0, tiled=True)  29.3 us
    dot_general x19, matrix products, dot(): return lax.dot_general(a, b, (dims, ((), ())), preferred_element_type=F32)  18.4 us
    all_to_all x2, waiting for transfers between devices, gather(): lax.all_to_all(jnp.broadcast_to(x[None], (n,) + x.shape), 'seq', 0, 0, ti...  17.2 us
    all_to_all x3, starting transfers between devices, scatter_sum(): got = lax.all_to_all(blocks, 'seq', 0, 0, tiled=True)  12 us
    unnamed x53, local copies, waits for them, and re-layouts  10.1 us
    all_to_all x2, starting transfers between devices, gather(): lax.all_to_all(jnp.broadcast_to(x[None], (n,) + x.shape), 'seq', 0, 0, ti...  8.83 us
    ppermute x1, starting transfers between devices, body(): prev = lax.ppermute(strain, 'seq', [(i, i + 1) for i in range(n - 1)])  4.87 us
    slice x1, local copies, waits for them, and re-layouts, body(): w1[channels:]  3.45 us
  transfers between devices with their start and end apart: 9, of which 5 were waited for; matrix products, arithmetic and copies ran while one was open for 24% of the time, Pallas kernels for 0%

profile of v1, /device:TPU:0, one launch (start us, length us, event | category | flops | bytes accessed | tf_op | source)
XLA Modules:
  0.0 135.8 jit_solution(13542986263795608338)
XLA Ops:
  0.6 4.9 %collective-permute-start = (f32[3,896]{1,0:T(4,128)}, f32[3,896]{1,0:T(4,128)S(1)}, u32[]{:S(2)}, u32[]{:S(2)}) collective-permute-start(f32[3,896]{1,0:T(4,128)} %param.8), channel_id=1, source_target_pairs={{0,2},{2,4},{4,6},{6,8},{8,10},{10,12},{12,14},{1,3},{3,5},{5,7},{... | collective-permute-start | bytes 32264 | tf_op jit(solution)/shard_map/ppermute | solution.py:63
  5.5 1.4 %fusion.92 = (s32[1]{0:T(128)}, s32[1]{0:T(128)}, s32[1]{0:T(128)}) fusion(s32[3]{0:T(128)} %param.9), kind=kLoop, calls=%fused_computation.159 | loop fusion | bytes 24 | tf_op jit(solution)/shard_map/slice | solution.py:66
  6.9 0.7 slice_bitcast_fusion
  7.6 0.7 reduce-precision_convert_fusion.3
  8.3 3.4 %fusion.87 = (bf16[1,512,2,256]{3,2,1,0:T(2,128)(2,1)}, bf16[1,512,2,256]{3,2,1,0:T(2,128)(2,1)S(1)}, bf16[1,512,2,256]{3,2,1,0:T(2,128)(2,1)S(1)}, bf16[1,512,2,256]{3,2,1,0:T(2,128)(2,1)}) fusion(bf16[2,1024,2,256]{3,2,1,0:T(2,128)(2,1)} %param.12), kind=kLoop, calls=%fused_computation.154 | loop fusion | bytes 4194304 | tf_op jit(solution)/shard_map/slice | solution.py:97
  11.9 0.7 copy-done.5
  12.8 0.2 fusion.74
  13.1 0.6 fusion.91
  19.8 0.6 convolution_add_fusion
  20.4 0.6 multiply_convert_fusion.2
  21.0 0.9 copy-done.12
  21.9 1.7 %convolution_convert_fusion = bf16[1408,512]{1,0:T(8,128)(2,1)} fusion(bf16[1408,256]{0,1:T(8,128)(2,1)S(1)} %multiply_convert_fusion.2, bf16[2,256,512]{2,1,0:T(8,128)(2,1)S(1)} %copy-done.18), kind=kOutput, calls=%fused_computation.5 | convolution fusion | flops 369819648 | bytes 2424832 | tf_op jit(solution)/shard_map/dot_general | solution.py:17
  26.1 1.1 copy.25
  27.2 1.9 %copy.24 = bf16[64,8,2,256]{3,1,2,0:T(8,128)(2,1)} copy(bf16[64,8,2,256]{3,2,1,0:T(2,128)(2,1)} %bitcast.81) | data formatting | bytes 1048576
  29.9 2.6 %multiply_convert_fusion.1 = bf16[1408,512]{1,0:T(8,128)(2,1)S(1)} fusion(bf16[1408,512]{1,0:T(8,128)(2,1)} %collective-permute-done.1, bf16[1408,512]{1,0:T(8,128)(2,1)} %convolution_convert_fusion, f32[1408]{0:T(1024)S(1)} %fusion.72, bf16[3,1408]{1,0:T(4,128)(2,1)S(1)} %slice.239, bf16[3,1408]{1,0:T(4,128)(2,1)S(1)} %slice.240, ...), kind=kOutput, calls=%fused_computation.12 | convolution fusion | flops 17405184 | bytes 4354048 | tf_op jit(solution)/shard_map/dot_general | solution.py:17
  32.5 0.8 fusion.20
  33.3 0.3 copy-done.2
  33.6 0.8 add_add_fusion
  34.4 0.4 copy-done.16
  34.9 0.7 subtract_multiply_fusion.3
  35.6 0.5 copy-done.14
  36.3 0.7 fusion.94
  37.1 0.3 copy-done.11
  37.4 0.3 copy-done
  37.7 0.7 fusion.93
  38.5 3.2 %fusion.3 = bf16[1408,512]{1,0:T(8,128)(2,1)} fusion(s32[]{:T(128)S(6)} %select_n.67, f32[512,512]{1,0:T(8,128)S(1)} %broadcast.104, f32[896,512]{1,0:T(8,128)S(1)} %fusion.94, f32[896,512]{1,0:T(8,128)S(1)} %fusion.93), kind=kLoop, calls=%fused_computation.9 | loop fusion | flops 2883584 | bytes 6160388 | tf_op jit(solution)/shard_map/convert_element_type | solution.py:114
  41.8 0.5 collective-permute-start.2
  42.3 3.0 %fusion.13 = bf16[256,512]{1,0:T(8,128)(2,1)} fusion(bf16[896,512]{1,0:T(8,128)(2,1)} %param.15, f32[896,512]{0,1:T(8,128)} %copy-done.14), kind=kOutput, calls=%fused_computation.33 | convolution fusion | flops 236290048 | bytes 3014656 | tf_op jit(solution)/shard_map/dot_general | solution.py:17
  45.3 4.9 %all-to-all-start.3 = ((bf16[8,32,512]{2,1,0:T(8,128)(2,1)}), bf16[8,32,512]{2,1,0:T(8,128)(2,1)S(1)}, u32[]{:S(2)}, u32[]{:S(2)}) async-start(bf16[8,32,512]{2,1,0:T(8,128)(2,1)} %bitcast.86), calls=%async_computation.3 | async-start | bytes 524288 | tf_op jit(solution)/shard_map/all_to_all | solution.py:43
  50.2 1.7 %fusion.6 = f32[512]{0:T(512)S(1)} fusion(f32[896,256]{0,1:T(8,128)} %copy-done.11, f32[896,256]{0,1:T(8,128)} %copy-done.10), kind=kLoop, calls=%fused_computation.18 | loop fusion | flops 916992 | bytes 1837056 | tf_op jit(solution)/shard_map/reduce_sum | solution.py:139
  51.9 2.4 %multiply_convert_fusion = bf16[1408,512]{1,0:T(8,128)(2,1)S(1)} fusion(bf16[1408,512]{1,0:T(8,128)(2,1)} %collective-permute-done.2, bf16[1408,512]{1,0:T(8,128)(2,1)} %fusion.3, bf16[896,512]{1,0:T(8,128)(2,1)S(1)} %copy-done.17, f32[1408]{0:T(1024)S(1)} %fusion.72), kind=kLoop, calls=%fused_computation.11 | loop fusion | flops 5767168 | bytes 5248512 | tf_op jit(solution)/shard_map/convert_element_type | solution.py:124
  54.3 0.3 fusion.49
  54.6 1.1 copy-done.20
  55.7 1.0 subtract_multiply_fusion.1
  56.8 0.5 fusion.11
  57.3 0.5 copy-done.8
  57.8 0.2 fusion.65
  58.0 0.3 convolution_add_fusion.2
  58.3 0.2 fusion.4
  58.6 0.7 all-to-all-done.3
  59.2 0.7 broadcast_in_dim.27
  60.0 5.3 %all-to-all-start = ((f32[8,11,512]{2,1,0:T(8,128)}), f32[8,11,512]{2,1,0:T(8,128)}, u32[]{:S(2)}, u32[]{:S(2)}) async-start(f32[8,11,512]{2,1,0:T(8,128)} %broadcast_in_dim.27), calls=%async_computation | async-start | bytes 524288 | tf_op jit(solution)/shard_map/all_to_all | solution.py:48
  65.3 2.8 %convolution_convert_fusion.3 = bf16[256,512]{1,0:T(8,128)(2,1)} fusion(bf16[1408,256]{0,1:T(8,128)(2,1)S(1)} %copy-done.13, bf16[1408,512]{1,0:T(8,128)(2,1)} %copy-done.4), kind=kOutput, calls=%fused_computation.34 | convolution fusion | flops 369229824 | bytes 2424832 | tf_op jit(solution)/shard_map/dot_general | solution.py:17
  68.1 5.8 %all-to-all-done = f32[8,11,512]{2,1,0:T(8,128)} async-done(((f32[8,11,512]{2,1,0:T(8,128)}), f32[8,11,512]{2,1,0:T(8,128)}, u32[]{:S(2)}, u32[]{:S(2)}) %all-to-all-start) | async-done | bytes 180256 | tf_op jit(solution)/shard_map/all_to_all | solution.py:48
  73.9 3.6 %all-to-all-start.2 = ((bf16[8,32,512]{2,1,0:T(8,128)(2,1)}), bf16[8,32,512]{2,1,0:T(8,128)(2,1)S(1)}, u32[]{:S(2)}, u32[]{:S(2)}) async-start(bf16[8,32,512]{2,1,0:T(8,128)(2,1)} %bitcast.87), calls=%async_computation.2 | async-start | bytes 524288 | tf_op jit(solution)/shard_map/all_to_all | solution.py:43
  77.5 0.8 convolution_convert_fusion.2
  78.3 0.8 convolution_convert_fusion.1
  79.1 1.0 pad_maximum_fusion.2
  80.1 5.9 %all-to-all-done.2 = bf16[8,32,512]{2,1,0:T(8,128)(2,1)S(1)} async-done(((bf16[8,32,512]{2,1,0:T(8,128)(2,1)}), bf16[8,32,512]{2,1,0:T(8,128)(2,1)S(1)}, u32[]{:S(2)}, u32[]{:S(2)}) %all-to-all-start.2) | async-done | bytes 262176 | tf_op jit(solution)/shard_map/all_to_all | solution.py:43
  86.0 0.7 copy-done.15
  86.7 3.6 %all-to-all-start.1 = ((bf16[8,128,512]{2,1,0:T(8,128)(2,1)}), bf16[8,128,512]{2,1,0:T(8,128)(2,1)S(1)}, u32[]{:S(2)}, u32[]{:S(2)}) async-start(bf16[8,128,512]{2,1,0:T(8,128)(2,1)} %bitcast.15), calls=%async_computation.1 | async-start | bytes 2097152 | tf_op jit(solution)/shard_map/all_to_all | solution.py:43
  90.3 0.7 constant_dynamic-slice_fusion
  91.0 1.0 reduce_sum.56
  92.1 1.0 reduce
  93.1 22.7 %all-to-all-done.1 = bf16[8,128,512]{2,1,0:T(8,128)(2,1)S(1)} async-done(((bf16[8,128,512]{2,1,0:T(8,128)(2,1)}), bf16[8,128,512]{2,1,0:T(8,128)(2,1)S(1)}, u32[]{:S(2)}, u32[]{:S(2)}) %all-to-all-start.1) | async-done | bytes 1048608 | tf_op jit(solution)/shard_map/all_to_all | solution.py:43
  115.8 0.8 broadcast_in_dim.28
  116.7 3.5 %all-to-all-start.4 = ((bf16[8,2,32,512]{3,2,1,0:T(8,128)(2,1)}), bf16[8,2,32,512]{3,2,1,0:T(8,128)(2,1)S(1)}, u32[]{:S(2)}, u32[]{:S(2)}) async-start(bf16[8,2,32,512]{3,2,1,0:T(8,128)(2,1)} %broadcast_in_dim.28), calls=%async_computation.4 | async-start | bytes 1048576 | tf_op jit(solution)/shard_map/all_to_all | solution.py:48
  120.2 0.6 reshape.162
  120.8 0.6 slice_select_fusion
  121.5 0.5 multiply_add_fusion
  122.1 0.2 stack.34
  122.3 1.0 pad_maximum_fusion.3
  123.3 11.4 %all-to-all-done.4 = bf16[8,2,32,512]{3,2,1,0:T(8,128)(2,1)S(1)} async-done(((bf16[8,2,32,512]{3,2,1,0:T(8,128)(2,1)}), bf16[8,2,32,512]{3,2,1,0:T(8,128)(2,1)S(1)}, u32[]{:S(2)}, u32[]{:S(2)}) %all-to-all-start.4) | async-done | bytes 524320 | tf_op jit(solution)/shard_map/all_to_all | solution.py:48
  134.7 1.1 copy_convert_fusion
  (78 shorter events, 1.8 us)
Async XLA Ops:
  0.6 18.8 %collective-permute-start = (f32[3,896]{1,0:T(4,128)}, f32[3,896]{1,0:T(4,128)S(1)}, u32[]{:S(2)}, u32[]{:S(2)}) collective-permute-start(f32[3,896]{1,0:T(4,128)} %param.8), channel_id=1, source_target_pairs={{0,2},{2,4},{4,6},{6,8},{8,10},{10,12},{12,14},{1,3},{3,5},{5,7},{... | collective-permute-start | bytes 32264 | tf_op jit(solution)/shard_map/ppermute | solution.py:63
  11.7 1.3 copy-start.22
  11.7 7.7 %copy-start.21 = (f32[3,896]{1,0:T(4,128)S(1)}, f32[3,896]{1,0:T(4,128)}, u32[]{:S(2)}) copy-start(f32[3,896]{1,0:T(4,128)} %param.8) | copy-start | bytes 32260
  11.8 0.8 copy-start.5
  11.9 0.9 copy-start.7
  20.4 1.5 %copy-start.18 = (bf16[2,256,512]{2,1,0:T(8,128)(2,1)S(1)}, bf16[2,256,512]{2,1,0:T(8,128)(2,1)}, u32[]{:S(2)}) copy-start(bf16[2,256,512]{2,1,0:T(8,128)(2,1)} %param.14) | copy-start | bytes 1572868
  21.0 0.9 copy-start.12
  23.6 6.3 %collective-permute-start.1 = (bf16[1408,512]{1,0:T(8,128)(2,1)}, bf16[1408,512]{1,0:T(8,128)(2,1)}, u32[]{:S(2)}, u32[]{:S(2)}) collective-permute-start(bf16[1408,512]{1,0:T(8,128)(2,1)} %convolution_convert_fusion), channel_id=1, source_target_pairs={{0,1},{1,0},{2,3},{3,2},{4,5},{5,4},{6,7},{7,6},{8,9},{9,8},{10,11... | collective-permute-start | bytes 4325384 | tf_op jit(solution)/shard_map/ppermute | solution.py:30
  29.8 2.6 %copy-start.9 = (bf16[64,8,2,256]{3,1,2,0:T(8,128)(2,1)S(1)}, bf16[64,8,2,256]{3,1,2,0:T(8,128)(2,1)}, u32[]{:S(2)}) copy-start(bf16[64,8,2,256]{3,1,2,0:T(8,128)(2,1)} %copy.24) | copy-start | bytes 1572868
  32.5 1.1 copy-start.2
  33.6 1.2 copy-start.16
  33.6 1.3 copy-start.19
  34.9 1.2 copy-start.14
  36.1 1.0 copy-start.10
  36.2 1.2 copy-start.11
  36.3 1.4 %copy-start = (bf16[896,512]{0,1:T(8,128)(2,1)}, bf16[896,512]{0,1:T(8,128)(2,1)S(1)}, u32[]{:S(2)}) copy-start(bf16[896,512]{0,1:T(8,128)(2,1)S(1)} %fusion.7) | copy-start | bytes 2752516
  41.8 10.1 %collective-permute-start.2 = (bf16[1408,512]{1,0:T(8,128)(2,1)}, bf16[1408,512]{1,0:T(8,128)(2,1)}, u32[]{:S(2)}, u32[]{:S(2)}) collective-permute-start(bf16[1408,512]{1,0:T(8,128)(2,1)} %fusion.3), channel_id=1, source_target_pairs={{0,1},{1,0},{2,3},{3,2},{4,5},{5,4},{6,7},{7,6},{8,9},{9,8},{10,11... | collective-permute-start | bytes 4325384 | tf_op jit(solution)/shard_map/ppermute | solution.py:30
  45.3 14.0 %all-to-all-start.3 = ((bf16[8,32,512]{2,1,0:T(8,128)(2,1)}), bf16[8,32,512]{2,1,0:T(8,128)(2,1)S(1)}, u32[]{:S(2)}, u32[]{:S(2)}) async-start(bf16[8,32,512]{2,1,0:T(8,128)(2,1)} %bitcast.86), calls=%async_computation.3 | async-start | bytes 524288 | tf_op jit(solution)/shard_map/all_to_all | solution.py:43
  50.2 1.7 %copy-start.17 = (bf16[896,512]{1,0:T(8,128)(2,1)S(1)}, bf16[896,512]{1,0:T(8,128)(2,1)}, u32[]{:S(2)}) copy-start(bf16[896,512]{1,0:T(8,128)(2,1)} %param.15) | copy-start | bytes 2752516
  54.3 2.5 %copy-start.4 = (bf16[1408,512]{1,0:T(8,128)(2,1)}, bf16[1408,512]{1,0:T(8,128)(2,1)S(1)}, u32[]{:S(2)}) copy-start(bf16[1408,512]{1,0:T(8,128)(2,1)S(1)} %multiply_convert_fusion) | copy-start | bytes 4325380
  54.3 1.4 %copy-start.20 = (bf16[2,256,512]{2,1,0:T(8,128)(2,1)S(1)}, bf16[2,256,512]{2,1,0:T(8,128)(2,1)}, u32[]{:S(2)}) copy-start(bf16[2,256,512]{2,1,0:T(8,128)(2,1)} %param.14) | copy-start | bytes 1572868
  56.8 1.0 copy-start.8
  56.8 1.3 copy-start.6
  58.3 7.0 %copy-start.13 = (bf16[1408,256]{0,1:T(8,128)(2,1)S(1)}, bf16[1408,256]{0,1:T(8,128)(2,1)}, u32[]{:S(2)}) copy-start(bf16[1408,256]{0,1:T(8,128)(2,1)} %copy-done.12) | copy-start | bytes 2162692
  60.0 14.0 %all-to-all-start = ((f32[8,11,512]{2,1,0:T(8,128)}), f32[8,11,512]{2,1,0:T(8,128)}, u32[]{:S(2)}, u32[]{:S(2)}) async-start(f32[8,11,512]{2,1,0:T(8,128)} %broadcast_in_dim.27), calls=%async_computation | async-start | bytes 524288 | tf_op jit(solution)/shard_map/all_to_all | solution.py:48
  65.3 12.2 %copy-start.1 = (bf16[896,512]{0,1:T(8,128)(2,1)S(1)}, bf16[896,512]{0,1:T(8,128)(2,1)}, u32[]{:S(2)}) copy-start(bf16[896,512]{0,1:T(8,128)(2,1)} %copy-done) | copy-start | bytes 2752516
  65.3 12.2 %copy-start.3 = (bf16[1408,512]{1,0:T(8,128)(2,1)S(1)}, bf16[1408,512]{1,0:T(8,128)(2,1)}, u32[]{:S(2)}) copy-start(bf16[1408,512]{1,0:T(8,128)(2,1)} %copy-done.2) | copy-start | bytes 4325380
  73.9 12.1 %all-to-all-start.2 = ((bf16[8,32,512]{2,1,0:T(8,128)(2,1)}), bf16[8,32,512]{2,1,0:T(8,128)(2,1)S(1)}, u32[]{:S(2)}, u32[]{:S(2)}) async-start(bf16[8,32,512]{2,1,0:T(8,128)(2,1)} %bitcast.87), calls=%async_computation.2 | async-start | bytes 524288 | tf_op jit(solution)/shard_map/all_to_all | solution.py:43
  86.0 0.7 copy-start.15
  86.7 29.1 %all-to-all-start.1 = ((bf16[8,128,512]{2,1,0:T(8,128)(2,1)}), bf16[8,128,512]{2,1,0:T(8,128)(2,1)S(1)}, u32[]{:S(2)}, u32[]{:S(2)}) async-start(bf16[8,128,512]{2,1,0:T(8,128)(2,1)} %bitcast.15), calls=%async_computation.1 | async-start | bytes 2097152 | tf_op jit(solution)/shard_map/all_to_all | solution.py:43
  92.0 28.8 %collective-permute-start.3 = (f32[3,512]{1,0:T(4,128)S(1)}, f32[3,512]{1,0:T(4,128)S(1)}, u32[]{:S(2)}, u32[]{:S(2)}) collective-permute-start(f32[3,512]{1,0:T(4,128)S(1)} %slice.260), channel_id=1, source_target_pairs={{0,1},{1,0},{2,3},{3,2},{4,5},{5,4},{6,7},{7,6},{8,9},{9,8},{10,11... | collective-permute-start | bytes 18440 | tf_op jit(solution)/shard_map/ppermute | solution.py:30
  116.7 18.1 %all-to-all-start.4 = ((bf16[8,2,32,512]{3,2,1,0:T(8,128)(2,1)}), bf16[8,2,32,512]{3,2,1,0:T(8,128)(2,1)S(1)}, u32[]{:S(2)}, u32[]{:S(2)}) async-start(bf16[8,2,32,512]{3,2,1,0:T(8,128)(2,1)} %broadcast_in_dim.28), calls=%async_computation.4 | async-start | bytes 1048576 | tf_op jit(solution)/shard_map/all_to_all | solution.py:48

commit v2 on v1

v2 whole, which is shorter than its diff:
```python
import functools
import math

import jax
import jax.numpy as jnp
from jax import lax
from jax.experimental import pallas as pl
from jax.experimental.pallas import tpu as pltpu
from jax.sharding import PartitionSpec as P

DET = 3
DILATION_EXPONENT = 9
MAXSHIFT = 128
LAG = 2**DILATION_EXPONENT
F32 = jnp.float32
BF16 = jnp.bfloat16
VMEM = pl.BlockSpec(memory_space=pltpu.VMEM)
SMEM = pl.BlockSpec(memory_space=pltpu.SMEM)


def dot(a, b, dims):
    return lax.dot_general(a, b, (dims, ((), ())), preferred_element_type=F32)


def swap(x):
    return lax.ppermute(x, "tensor", [(0, 1), (1, 0)])


def halves(x):
    hi = x.astype(BF16).astype(F32)
    return hi, x - hi


def gates(filt, gate):
    return jnp.tanh(filt), 0.5 * jnp.tanh(0.5 * gate) + 0.5


def taps(x, w, layer, half, rows):
    sl = slice(half * rows, (half + 1) * rows)
    return [dot(x, w[layer, g, sl, :], ((1,), (0,))) for g in range(2)]


def untaps(gl, w, layer, half, rows):
    width = w.shape[3]
    sl = slice(half * rows, (half + 1) * rows)
    return dot(gl[:, :width], w[layer, 0, sl, :], ((1,), (1,))) + dot(
        gl[:, width:], w[layer, 1, sl, :], ((1,), (1,))
    )


def rows8(x):
    return sum(x[i : i + 8] for i in range(0, x.shape[0], 8))


def row_tiles(ext):
    return [(0, LAG)] + [(at, min(512, ext - at)) for at in range(LAG, ext, 512)]


def first_layer(offs, dil, prev, own, iw, w, bias, ow, mine, gate0, fa, fb, st, srow, i3, line, sig):
    rows = own.shape[1]
    channels = iw.shape[1]
    width = ow.shape[1]
    ext = rows + LAG
    full = line.shape[1]
    spare = full - 2 * rows
    line[...] = jnp.zeros_like(line)
    line[0:DET, spare : spare + rows] = prev[...]
    line[0:DET, spare + rows :] = own[...]
    sig[...] = jnp.zeros_like(sig)
    for k in range(DET):
        at = LAG + MAXSHIFT - offs[k]
        for j, start in ((k, at - dil[0]), (DET + k, at)):
            moved = pltpu.roll(line[...], full - start, 1)
            sig[j : j + 1, :] = moved[k : k + 1, :ext]
    s_hi, s_lo = halves(sig[...])
    stack = jnp.concatenate([s_hi, s_lo, s_hi, jnp.zeros_like(s_hi)], axis=0)
    srow[...] = stack[:16].astype(BF16)
    st[...] = stack.T.astype(BF16)

    i_hi, i_lo = halves(iw[...])
    pad2 = jnp.zeros((2, channels), F32)
    pad3 = jnp.zeros((3, channels), F32)
    pad8 = jnp.zeros((8, channels), F32)
    i3[...] = jnp.concatenate(
        [pad3, i_hi, pad2, pad3, i_hi, pad2, pad3, i_lo, pad2, pad8], axis=0
    ).astype(BF16)
    i2 = jnp.concatenate([i_hi, i_lo, pad2, pad8], axis=0).astype(BF16)
    a_lag = jnp.concatenate(taps(i2, w, 0, 0, channels), axis=1)
    a_cur = jnp.concatenate(taps(i2, w, 0, 1, channels), axis=1)
    a0 = jnp.concatenate(
        [a_lag[:DET] + a_lag[DET : 2 * DET], a_cur[:DET] + a_cur[DET : 2 * DET], pad2[:, : 2 * width]], axis=0
    )
    a_hi, a_lo = halves(a0)
    a3 = jnp.concatenate([a_hi, a_hi, a_lo, jnp.zeros_like(a_hi)], axis=0).astype(BF16)
    for at, size in row_tiles(ext):
        sl = slice(at, at + size)
        pre = dot(st[sl, :], a3, ((1,), (0,)))
        th, sg = gates(pre[:, :width] + bias[0, 0:1, :], pre[:, width:] + bias[0, 1:2, :])
        gate = th * sg
        fa[sl, :] = sg - gate * th
        fb[sl, :] = gate - gate * sg
        gate = gate.astype(BF16)
        gate0[sl, :] = gate
        mine[sl, :] = dot(gate, ow[0], ((1,), (0,))).astype(BF16)


def second_layer(
    scale, dil, mine, other, st, i3, w, bias, ow, cot, part, gl1, gate1, joined, bias1, h1, acc, moved, pre, gg
):
    rows, channels = cot.shape
    width = ow.shape[1]
    ext = rows + LAG
    d = dil[1]
    inside = jnp.where(lax.axis_index("seq") == 0, 0.0, 1.0)

    def hidden(i, carry):
        sl = pl.ds(pl.multiple_of(i * 128, 128), 128)
        h = dot(st[sl, :], i3[...], ((1,), (0,)))
        h = h + mine[sl, :].astype(F32) + other[sl, :].astype(F32)
        h1[sl, :] = h * jnp.where(i * 128 < LAG, inside, 1.0)
        return carry

    lax.fori_loop(0, ext // 128, hidden, 0)
    near = LAG - pl.multiple_of((d // 8) * 8, 8)

    @pl.when(d >= 8)
    def _():
        joined[:, :channels] = h1[pl.ds(pl.multiple_of(near, 8), rows), :].astype(BF16)

    @pl.when(d < 8)
    def _():
        joined[:, :channels] = pltpu.roll(h1[LAG - 8 :, :], d, 0)[8:].astype(BF16)

    joined[:, channels:] = h1[LAG:, :].astype(BF16)
    for g in range(2):
        pre[:, g * width : (g + 1) * width] = dot(joined[...], w[1, g], ((1,), (0,)))
    gg[...] = dot(cot[...], ow[1], ((1,), (1,)))

    def local(i, total):
        sl = pl.ds(pl.multiple_of(i * 32, 32), 32)
        th, sg = gates(pre[sl, :width] + bias[1, 0:1, :], pre[sl, width:] + bias[1, 1:2, :])
        gate = th * sg
        gate1[sl, :] = gate.astype(BF16)
        up = gg[sl, :] * scale
        gf = up * (sg - gate * th)
        gs = up * (gate - gate * sg)
        gl1[sl, :width] = gf.astype(BF16)
        gl1[sl, width:] = gs.astype(BF16)
        return total[0] + rows8(gf), total[1] + rows8(gs)

    zero = jnp.zeros((8, width), F32)
    tf, ts = lax.fori_loop(0, rows // 32, local, (zero, zero))
    bias1[:, :width] = jnp.sum(tf, axis=0, keepdims=True)
    bias1[:, width:] = jnp.sum(ts, axis=0, keepdims=True)
    acc[:LAG, :] = jnp.zeros((LAG, channels), F32)
    moved[:8, :] = jnp.zeros((8, channels), F32)
    acc[LAG:, :] = untaps(gl1[...], w, 1, 1, channels)
    moved[8:, :] = untaps(gl1[...], w, 1, 0, channels)

    @pl.when(d >= 8)
    def _():
        acc[pl.ds(pl.multiple_of(near, 8), rows), :] += moved[8:, :]

    @pl.when(d < 8)
    def _():
        acc[LAG - 8 :, :] += pltpu.roll(moved[...], rows + 8 - d, 0)

    part[...] = acc[...].astype(BF16)


def first_back(
    scale, part, apart, cot, gate0, fa, fb, srow, ow, w, bias1, do1, *refs
):
    outs, (adj_s, gl_s, out_s, gg) = refs[:-4], refs[-4:]
    rows, channels = cot.shape
    width = ow.shape[1]
    ext = rows + LAG
    inside = jnp.where(lax.axis_index("seq") == 0, 0.0, 1.0)
    first = jnp.where(lax.axis_index("tensor") == 0, 1.0, 0.0)
    adj_s[:LAG, :] = ((part[:LAG, :].astype(F32) + apart[:LAG, :].astype(F32)) * inside).astype(BF16)
    adj_s[LAG:, :] = (
        part[LAG:, :].astype(F32) + apart[LAG:, :].astype(F32) + cot[...].astype(F32) * scale
    ).astype(BF16)
    gg[...] = dot(adj_s[...], ow[0], ((1,), (1,)))

    def local(i, total):
        sl = pl.ds(pl.multiple_of(i * 64, 64), 64)
        gf = gg[sl, :] * fa[sl, :]
        gs = gg[sl, :] * fb[sl, :]
        gl_s[sl, :width] = gf.astype(BF16)
        gl_s[sl, width:] = gs.astype(BF16)
        return total[0] + rows8(gf), total[1] + rows8(gs)

    zero = jnp.zeros((8, width), F32)
    tf, ts = lax.fori_loop(0, ext // 64, local, (zero, zero))
    bias = jnp.concatenate([jnp.sum(tf, axis=0, keepdims=True), jnp.sum(ts, axis=0, keepdims=True)], axis=1)
    out_s[...] = dot(gate0[...], adj_s[...], ((0,), (0,))).reshape(out_s.shape)
    r2 = dot(srow[...], gl_s[...], ((1,), (0,)))
    g2 = dot(srow[...], adj_s[...], ((1,), (0,)))
    r = r2[:8] + r2[8:]
    g = (g2[:8] + g2[8:]) * first
    r_hi, r_lo = halves(r)
    rr = jnp.concatenate([r_hi, r_lo], axis=0).astype(BF16)
    b_lag = untaps(rr, w, 0, 0, channels)
    b_cur = untaps(rr, w, 0, 1, channels)
    b_lag = b_lag[:8] + b_lag[8:]
    b_cur = b_cur[:8] + b_cur[8:]
    g = g[DET : 2 * DET] + b_lag[:DET] + b_cur[DET : 2 * DET]
    small = jnp.concatenate(
        [r[: 2 * DET], g, bias, bias1[...], jnp.zeros((5, 2 * width), F32)], axis=0
    )
    if len(outs) == 2:
        outs[0][...] = out_s[...].reshape(outs[0].shape)
        outs[1][...] = small
    else:
        m = out_s.shape[1]
        outs[0][:, :m, :] = out_s[...].astype(BF16)
        outs[0][:, m : 2 * m, :] = do1[...].reshape(out_s.shape)
        outs[0][:, 2 * m :, :] = jnp.broadcast_to(small.astype(BF16)[None], (8,) + small.shape)


def out_grad(scale, gate1, cot, out):
    out[...] = (dot(gate1[...], cot[...], ((0,), (0,))) * scale).astype(BF16)


def conv_grad(joined, gl1, keep, send, full):
    x = lax.axis_index("seq") & 1
    full[...] = dot(joined[...], gl1[...], ((0,), (0,))).reshape(full.shape)
    for z in range(4):
        keep[z] = full[2 * z + x]
        send[z] = full[2 * z + 1 - x].astype(BF16)


def pair_add(keep, got, own, send):
    z = lax.axis_index("seq") >> 1
    for k, ref, i in ((0, own, 0), (2, own, 1), (1, send, 0), (3, send, 1)):
        ref[i] = (keep[z ^ k] + got[z ^ k].astype(F32)).astype(ref.dtype)


def pair_add_again(keep, got, own, send):
    own[...] = keep[0] + got[0].astype(F32)
    send[...] = (keep[1] + got[1].astype(F32)).astype(BF16)


def sum_blocks(got, blocks, small):
    m = blocks.shape[1]
    total = got[0].astype(F32)
    for k in range(1, 8):
        total = total + got[k].astype(F32)
    small[...] = total[m:]
    both = total[:m].astype(BF16)
    for k in range(8):
        blocks[k] = both


def scatter_sum(x, n):
    blocks = x.astype(BF16).reshape(n, x.shape[0] // n, x.shape[1])
    got = lax.all_to_all(blocks, "seq", 0, 0, tiled=True)
    return jnp.sum(got.astype(F32), axis=0)


def gather(x, n):
    return lax.all_to_all(jnp.broadcast_to(x[None], (n,) + x.shape), "seq", 0, 0, tiled=True)


def along(x, k):
    n = lax.axis_size("seq")
    return lax.ppermute(x, "seq", [(i, i ^ k) for i in range(n)])


def shape(dims, dtype):
    return jax.ShapeDtypeStruct(dims, dtype)


def all_to_all(x):
    return lax.all_to_all(x, "seq", 0, 0, tiled=True)


def pair_shapes(lead, m, channels):
    dims = (lead, m, channels) if lead else (m, channels)
    return [shape(dims, F32), shape(dims, BF16)]


def limit(mib):
    return pltpu.CompilerParams(vmem_limit_bytes=mib * 2**20)


def call(kernel, out_shape, scratch=()):
    def run(*args):
        count = len(out_shape) if isinstance(out_shape, list) else 0
        return pl.pallas_call(
            kernel,
            out_shape=out_shape,
            in_specs=[VMEM] * len(args),
            out_specs=[VMEM] * count if count else VMEM,
            scratch_shapes=list(scratch),
            compiler_params=limit(8),
            name=getattr(kernel, "func", kernel).__name__,
        )(*args)

    return run


def body(strain, offsets, dilation, input_weight, conv_weight, conv_bias, out_weight, cotangent):
    rows = strain.shape[1]
    channels = input_weight.shape[1]
    width = conv_weight.shape[3]
    n = lax.axis_size("seq")
    me = lax.axis_index("seq")
    ext = LAG + rows
    scale = 1.0 / math.sqrt(rows * n)
    prev = lax.ppermute(strain, "seq", [(i, i + 1) for i in range(n - 1)])
    weight = jnp.transpose(conv_weight, (0, 2, 1, 3))
    full = ext + LAG + MAXSHIFT
    mine, gate0, fa, fb, st, srow, i3 = pl.pallas_call(
        first_layer,
        out_shape=[
            shape((ext, channels), BF16),
            shape((ext, width), BF16),
            shape((ext, width), F32),
            shape((ext, width), F32),
            shape((ext, 32), BF16),
            shape((16, ext), BF16),
            shape((32, channels), BF16),
        ],
        in_specs=[SMEM, SMEM] + [VMEM] * 6,
        out_specs=[VMEM] * 7,
        scratch_shapes=[pltpu.VMEM((8, full), F32), pltpu.VMEM((8, ext), F32)],
        compiler_params=limit(10),
        name="first_layer",
    )(offsets, dilation, prev, strain, input_weight, weight, conv_bias, out_weight)
    other = swap(mine)
    part, gl1, gate1, joined, bias1 = pl.pallas_call(
        functools.partial(second_layer, scale),
        out_shape=[
            shape((ext, channels), BF16),
            shape((rows, 2 * width), BF16),
            shape((rows, width), BF16),
            shape((rows, 2 * channels), BF16),
            shape((1, 2 * width), F32),
        ],
        in_specs=[SMEM] + [VMEM] * 8,
        out_specs=[VMEM] * 5,
        scratch_shapes=[
            pltpu.VMEM((ext, channels), F32),
            pltpu.VMEM((ext, channels), F32),
            pltpu.VMEM((rows + 8, channels), F32),
            pltpu.VMEM((rows, 2 * width), F32),
            pltpu.VMEM((rows, width), F32),
        ],
        compiler_params=limit(28),
        name="second_layer",
    )(dilation, mine, other, st, i3, weight, conv_bias, out_weight, cotangent)
    apart = swap(part)

    if n == 8:
        c_keep, c_send = call(
            conv_grad,
            [shape((4, channels // 4, 2 * width), F32), shape((4, channels // 4, 2 * width), BF16)],
            [pltpu.VMEM((8, channels // 4, 2 * width), F32)],
        )(joined, gl1)
        c_got = along(c_send, 1)
    do1 = call(functools.partial(out_grad, scale), shape((width, channels), BF16))(gate1, cotangent)
    m = width // n
    if n == 8:
        back_shapes = [shape((n, 2 * m + 16, channels), BF16)]
        held = (n, m, channels)
    else:
        back_shapes = [shape((width, channels), F32), shape((16, 2 * width), F32)]
        held = (width, channels)
    back = pl.pallas_call(
        functools.partial(first_back, scale),
        out_shape=back_shapes,
        in_specs=[VMEM] * 11,
        out_specs=[VMEM] * len(back_shapes),
        scratch_shapes=[
            pltpu.VMEM((ext, channels), BF16),
            pltpu.VMEM((ext, 2 * width), BF16),
            pltpu.VMEM(held, F32),
            pltpu.VMEM((ext, width), F32),
        ],
        compiler_params=limit(16),
        name="first_back",
    )(part, apart, cotangent, gate0, fa, fb, srow, out_weight, weight, bias1, do1)
    if n == 8:
        back_got = all_to_all(back[0])
        c_two, c_send = call(pair_add, pair_shapes(2, channels // 4, 2 * width))(c_keep, c_got)
        c_got = along(c_send, 2)
        blocks, small = call(
            sum_blocks, [shape((n, 2 * m, channels), BF16), shape((16, channels), F32)]
        )(back_got)
        do = all_to_all(blocks)
        c_own, c_send = call(pair_add_again, pair_shapes(0, channels // 4, 2 * width))(c_two, c_got)
        c_got = along(c_send, 4)
        dw1 = c_own + c_got.astype(F32)
        do = jnp.transpose(do.reshape(n, 2, m, channels), (1, 0, 2, 3)).astype(F32)
        grad_out = do.reshape(2, width, channels)
    else:
        dw1 = scatter_sum(dot(joined, gl1, ((0,), (0,))), n)
        do1 = scatter_sum(do1, n)
        do0 = scatter_sum(back[0], n)
        small = jnp.sum(gather(back[1], n), axis=0)
        do = gather(jnp.stack([do0, do1]).astype(BF16), n).astype(F32)
        grad_out = jnp.moveaxis(do, 0, 1).reshape(2, width, channels)
    r, g, bias = small[: 2 * DET], small[2 * DET : 3 * DET], small[3 * DET : 3 * DET + 2]
    grad_input = g + swap(g)
    grad_bias = bias.reshape(2, 2, width)
    block = 2 * channels // n
    mine_iw = lax.dynamic_slice_in_dim(input_weight, (me * block) % channels, block, 1)
    mine_r = jnp.where(me * block < channels, r[:DET], r[DET:])
    dw0 = sum(mine_iw[k][:, None] * mine_r[k][None, :] for k in range(DET))
    grad_conv = jnp.stack([dw0, dw1]).reshape(2, block, 2, width)
    return (grad_input, grad_conv, grad_bias, grad_out)


def solution(mesh):
    in_specs = (
        P(None, ("groups", "seq")),
        P("groups"),
        P(),
        P(),
        P(None, None, None, "tensor"),
        P(None, None, "tensor"),
        P(None, "tensor", None),
        P(("groups", "seq"), None),
    )
    out_specs = (
        P("groups", None),
        P("groups", "seq", None, "tensor"),
        P("groups", None, "tensor"),
        P("groups", "tensor", None),
    )
    return jax.shard_map(body, mesh=mesh, in_specs=in_specs, out_specs=out_specs, check_vma=False)
```

time: 137 us -> 86.6 us (0.63)
  matrix products: 18.4 us -> 0 us
  local copies, waits for them, and re-layouts: 19.1 us -> 3.83 us
  Pallas kernels: 0 us -> 15.1 us
  other arithmetic: 15.5 us -> 2.26 us
  between operations: 10.1 us -> 0.86 us
  starting transfers between devices: 26.3 us -> 21.3 us
  waiting for transfers between devices: 46.5 us -> 41.9 us
    all_to_all x5 -> x2, waiting for transfers between devices: 46.5 us -> 11.2 us  [all_to_all(): return lax.all_to_all(x, 'seq', 0, 0, tiled=True)]
    ppermute x0 -> x3, waiting for transfers between devices: none -> 24.9 us  [along(): return lax.ppermute(x, 'seq', [(i, i ^ k) for i in range(n)])]
    dot_general x19 -> x0, matrix products: 18.4 us -> none  [dot(): return lax.dot_general(a, b, (dims, ((), ())), preferred_element_type=F32)]
    pallas_call x0 -> x8, Pallas kernels: none -> 15.1 us  [the longest x1 6.18 us: body(): pl.pallas_call(functools.partial(second_layer, scale), out_shape=[shape((...]
    all_to_all x5 -> x2, starting transfers between devices: 20.8 us -> 9.82 us  [all_to_all(): return lax.all_to_all(x, 'seq', 0, 0, tiled=True)]
    unnamed x53 -> x15, local copies, waits for them, and re-layouts: 10.1 us -> 1.9 us
    convert_element_type x9 -> x0, other arithmetic: 7.08 us -> none  [the longest x1 3.24 us: body(): part = (base + moved).astype(BF16)]
    ppermute x0 -> x3, starting transfers between devices: none -> 6.21 us  [along(): return lax.ppermute(x, 'seq', [(i, i ^ k) for i in range(n)])]
  transfers between devices with their start and end apart: 9 -> 9, of which waited for: 5 -> 6; matrix products, arithmetic and copies ran while one was open for 24% -> 6% of each run, Pallas kernels for 0% -> 3%
where the time goes in v2:
time: 86.6 us; the launch traced here: 85.2 us
  waiting for transfers between devices  41.9 us (48%)
  starting transfers between devices  21.3 us (25%)
  Pallas kernels  15.1 us (17%)
  local copies, waits for them, and re-layouts  3.83 us (4%)
  other arithmetic  2.26 us (3%)
    ppermute x3, waiting for transfers between devices, along(): return lax.ppermute(x, 'seq', [(i, i ^ k) for i in range(n)])  24.9 us
    all_to_all x2, waiting for transfers between devices, all_to_all(): return lax.all_to_all(x, 'seq', 0, 0, tiled=True)  11.2 us
    all_to_all x2, starting transfers between devices, all_to_all(): return lax.all_to_all(x, 'seq', 0, 0, tiled=True)  9.82 us
    ppermute x3, starting transfers between devices, along(): return lax.ppermute(x, 'seq', [(i, i ^ k) for i in range(n)])  6.21 us
    pallas_call x1, Pallas kernels, body(): pl.pallas_call(functools.partial(second_layer, scale), out_shape=[shape((...  6.18 us
    ppermute x3, waiting for transfers between devices, swap(): return lax.ppermute(x, 'tensor', [(0, 1), (1, 0)])  5.83 us
    ppermute x1, starting transfers between devices, body(): prev = lax.ppermute(strain, 'seq', [(i, i + 1) for i in range(n - 1)])  5 us
    pallas_call x1, Pallas kernels, body(): pl.pallas_call(functools.partial(first_back, scale), out_shape=back_shape...  3.84 us
  transfers between devices with their start and end apart: 9, of which 6 were waited for; matrix products, arithmetic and copies ran while one was open for 6% of the time, Pallas kernels for 3%

profile of v2, /device:TPU:0, one launch (start us, length us, event | category | flops | bytes accessed | tf_op | source)
XLA Modules:
  0.0 85.2 jit_solution(17108492628139170841)
XLA Ops:
  0.6 0.0 copy-start.3
  0.6 0.0 copy-start.5
  0.7 0.0 copy-start.4
  0.7 0.0 copy-start.2
  0.7 0.0 copy-start.1
  0.7 0.0 copy-start.6
  0.7 5.0 %collective-permute-start = (f32[3,896]{1,0:T(4,128)}, f32[3,896]{1,0:T(4,128)S(1)}, u32[]{:S(2)}, u32[]{:S(2)}) collective-permute-start(f32[3,896]{1,0:T(4,128)} %own.1), channel_id=1, source_target_pairs={{0,2},{2,4},{4,6},{6,8},{8,10},{10,12},{12,14},{1,3},{3,5},{5,7},{... | collective-permute-start | bytes 32264 | tf_op jit(solution)/shard_map/ppermute | solution.py:312
  5.7 1.9 %copy.15 = bf16[2,1024,2,256]{3,1,2,0:T(8,128)(2,1)S(1)} copy(bf16[2,1024,2,256]{3,2,1,0:T(2,128)(2,1)} %param.12) | data formatting | bytes 4194304 | tf_op args[4]
  7.6 0.0 copy-start
  7.6 0.0 collective-permute-done.prev
  7.6 0.0 copy-done.3
  7.6 0.0 copy-done.5
  7.6 0.0 copy-done.4
  7.6 0.0 copy-done.2
  7.6 0.0 copy-done.1
  7.6 0.0 copy-done.6
  7.7 2.1 %first_layer.1 = (bf16[1408,512]{1,0:T(8,128)(2,1)S(1)}, bf16[1408,256]{1,0:T(8,128)(2,1)S(1)}, f32[1408,256]{1,0:T(8,128)S(1)}, f32[1408,256]{1,0:T(8,128)S(1)}...) custom-call(s32[3]{0:T(128)S(1)} %copy-done.6, s32[2]{0:T(128)S(1)} %copy-done.5, ...), custom_call_target="tpu_custom_call" | custom-call | tf_op jit(solution)/shard_map/first_layer/pallas_call | solution.py:315
  9.8 0.1 collective-permute-start.1
  9.8 3.2 %collective-permute-done.1.other = bf16[1408,512]{1,0:T(8,128)(2,1)S(1)} collective-permute-done((bf16[1408,512]{1,0:T(8,128)(2,1)S(1)}, bf16[1408,512]{1,0:T(8,128)(2,1)S(1)}, u32[]{:S(2)}, u32[]{:S(2)}) %collective-permute-start.1) | collective-permute-done | bytes 1441824 | tf_op jit(solution)/shard_map/ppermute | solution.py:26
  13.0 0.0 copy-done
  13.0 6.2 %second_layer.1 = (bf16[1408,512]{1,0:T(8,128)(2,1)S(1)}, bf16[896,512]{1,0:T(8,128)(2,1)S(1)}, bf16[896,256]{1,0:T(8,128)(2,1)S(1)}, bf16[896,1024]{1,0:T(8,128)(2,1)S(1)}, f32[1,512]{1,0:T(1,128)S(1)}) custom-call(s32[2]{0:T(128)S(1)} %copy-done.5, bf16[1408,512]{1,0:T(8,128)(2,1)S(1)} %get-tuple-element.24.mine, ...), custom_call_target="tpu_custom_call" | custom-call | tf_op jit(solution)/shard_map/second_layer/pallas_call | solution.py:333
  19.2 0.2 collective-permute-start.2
  19.4 0.5 out_grad.1.do1
  19.9 2.6 %collective-permute-done.2.apart = bf16[1408,512]{1,0:T(8,128)(2,1)S(1)} collective-permute-done((bf16[1408,512]{1,0:T(8,128)(2,1)S(1)}, bf16[1408,512]{1,0:T(8,128)(2,1)S(1)}, u32[]{:S(2)}, u32[]{:S(2)}) %collective-permute-start.2) | collective-permute-done | bytes 1441824 | tf_op jit(solution)/shard_map/ppermute | solution.py:26
  22.5 3.8 %first_back.1 = bf16[8,80,512]{2,1,0:T(8,128)(2,1)} custom-call(bf16[1408,512]{1,0:T(8,128)(2,1)S(1)} %get-tuple-element.27.part, bf16[1408,512]{1,0:T(8,128)(2,1)S(1)} %collective-permute-done.2.apart, bf16[896,512]{1,0:T(8,128)(2,1)S(1)} %copy-done, bf16[1408,256]{1,0:T(8,128)(2,1)S(1)} %get-tuple-element.28.gate0, f32[1408,256]{1,0:T(8,128)S(1)} %get-tuple-element.29.fa, ...), custom_call_target="tpu_custom_call" | custom-call | tf_op jit(solution)/shard_map/first_back/pallas_call | solution.py:371
  26.4 6.3 %all-to-all-start = ((bf16[8,80,512]{2,1,0:T(8,128)(2,1)}), bf16[8,80,512]{2,1,0:T(8,128)(2,1)S(1)}, u32[]{:S(2)}, u32[]{:S(2)}) async-start(bf16[8,80,512]{2,1,0:T(8,128)(2,1)} %first_back.1), calls=%async_computation | async-start | bytes 1310720 | tf_op jit(solution)/shard_map/all_to_all | solution.py:276
  32.7 1.5 %conv_grad.1 = (f32[4,128,512]{2,1,0:T(8,128)S(1)}, bf16[4,128,512]{2,1,0:T(8,128)(2,1)S(1)}) custom-call(bf16[896,1024]{1,0:T(8,128)(2,1)S(1)} %get-tuple-element.35.joined, bf16[896,512]{1,0:T(8,128)(2,1)S(1)} %get-tuple-element.36.gl1), custom_call_target="tpu_custom_call" | custom-call | tf_op jit(solution)/shard_map/conv_grad/pallas_call | solution.py:291
  34.2 2.1 %collective-permute-start.4 = (bf16[4,128,512]{2,1,0:T(8,128)(2,1)S(1)}, bf16[4,128,512]{2,1,0:T(8,128)(2,1)S(1)}, u32[]{:S(2)}, u32[]{:S(2)}) collective-permute-start(bf16[4,128,512]{2,1,0:T(8,128)(2,1)S(1)} %get-tuple-element.38), channel_id=1, source_target_pairs={{0,2},{2,0},{4,6},{6,4},{8,10},{10,8},{12,14},{14,12},{1,3},{3,1},... | collective-permute-start | bytes 1572872 | tf_op jit(solution)/shard_map/ppermute | solution.py:268
  36.3 17.6 %collective-permute-done.4.got = bf16[4,128,512]{2,1,0:T(8,128)(2,1)S(1)} collective-permute-done((bf16[4,128,512]{2,1,0:T(8,128)(2,1)S(1)}, bf16[4,128,512]{2,1,0:T(8,128)(2,1)S(1)}, u32[]{:S(2)}, u32[]{:S(2)}) %collective-permute-start.4) | collective-permute-done | bytes 524320 | tf_op jit(solution)/shard_map/ppermute | solution.py:268
  53.8 0.1 pair_add.1
  53.9 1.5 %collective-permute-start.5 = (bf16[2,128,512]{2,1,0:T(8,128)(2,1)S(1)}, bf16[2,128,512]{2,1,0:T(8,128)(2,1)S(1)}, u32[]{:S(2)}, u32[]{:S(2)}) collective-permute-start(bf16[2,128,512]{2,1,0:T(8,128)(2,1)S(1)} %get-tuple-element.40), channel_id=1, source_target_pairs={{0,4},{2,6},{4,0},{6,2},{8,12},{10,14},{12,8},{14,10},{1,5},{3,7},... | collective-permute-start | bytes 786440 | tf_op jit(solution)/shard_map/ppermute | solution.py:268
  55.4 6.2 %collective-permute-done.5.got = bf16[2,128,512]{2,1,0:T(8,128)(2,1)S(1)} collective-permute-done((bf16[2,128,512]{2,1,0:T(8,128)(2,1)S(1)}, bf16[2,128,512]{2,1,0:T(8,128)(2,1)S(1)}, u32[]{:S(2)}, u32[]{:S(2)}) %collective-permute-start.5) | collective-permute-done | bytes 262176 | tf_op jit(solution)/shard_map/ppermute | solution.py:268
  61.7 2.6 %collective-permute-start.6 = (bf16[128,512]{1,0:T(8,128)(2,1)S(1)}, bf16[128,512]{1,0:T(8,128)(2,1)S(1)}, u32[]{:S(2)}, u32[]{:S(2)}) collective-permute-start(bf16[128,512]{1,0:T(8,128)(2,1)S(1)} %get-tuple-element.42), channel_id=1, source_target_pairs={{0,8},{2,10},{4,12},{6,14},{8,0},{10,2},{12,4},{14,6},{1,9},{3,11}... | collective-permute-start | bytes 393224 | tf_op jit(solution)/shard_map/ppermute | solution.py:268
  64.3 0.0 all-to-all-done.got
  64.3 0.9 %sum_blocks.1 = (bf16[8,64,512]{2,1,0:T(8,128)(2,1)}, f32[16,512]{1,0:T(8,128)S(1)}) custom-call(bf16[8,80,512]{2,1,0:T(8,128)(2,1)S(1)} %all-to-all-done.got), custom_call_target="tpu_custom_call" | custom-call | tf_op jit(solution)/shard_map/sum_blocks/pallas_call | solution.py:291
  65.2 0.0 collective-permute-start.3
  65.2 3.5 %all-to-all-start.1 = ((bf16[8,64,512]{2,1,0:T(8,128)(2,1)}), bf16[8,64,512]{2,1,0:T(8,128)(2,1)S(1)}, u32[]{:S(2)}, u32[]{:S(2)}) async-start(bf16[8,64,512]{2,1,0:T(8,128)(2,1)} %get-tuple-element.43), calls=%async_computation.1 | async-start | bytes 1048576 | tf_op jit(solution)/shard_map/all_to_all | solution.py:276
  68.7 1.1 %collective-permute-done.6 = bf16[128,512]{1,0:T(8,128)(2,1)S(1)} collective-permute-done((bf16[128,512]{1,0:T(8,128)(2,1)S(1)}, bf16[128,512]{1,0:T(8,128)(2,1)S(1)}, u32[]{:S(2)}, u32[]{:S(2)}) %collective-permute-start.6) | collective-permute-done | bytes 131104 | tf_op jit(solution)/shard_map/ppermute | solution.py:268
  69.8 0.2 stack.7
  70.0 0.6 reshape.99
  70.6 0.0 collective-permute-done.3
  70.6 0.6 slice_select_fusion
  71.3 0.5 multiply_add_fusion
  71.8 1.0 %pad_maximum_fusion = f32[2,128,2,256]{3,2,1,0:T(2,128)} fusion(f32[1,128,2,256]{3,2,1,0:T(2,128)S(1)} %stack.7, f32[1,128,2,256]{3,2,1,0:T(2,128)S(1)} %multiply_add_fusion), kind=kLoop, calls=%fused_computation.2 | loop fusion | flops 131072 | bytes 1048576 | tf_op jit(solution)/shard_map/stack | solution.py:412
  72.8 11.2 %all-to-all-done.1 = bf16[8,64,512]{2,1,0:T(8,128)(2,1)S(1)} async-done(((bf16[8,64,512]{2,1,0:T(8,128)(2,1)}), bf16[8,64,512]{2,1,0:T(8,128)(2,1)S(1)}, u32[]{:S(2)}, u32[]{:S(2)}) %all-to-all-start.1) | async-done | bytes 524320 | tf_op jit(solution)/shard_map/all_to_all | solution.py:276
  84.1 0.1 convert_bitcast_fusion
  84.2 1.1 %copy.13 = f32[2,8,32,512]{3,2,1,0:T(8,128)} copy(f32[2,8,32,512]{3,2,0,1:T(8,128)S(1)} %convert_bitcast_fusion) | data formatting | bytes 2097152 | tf_op jit(solution)/shard_map/reshape | solution.py:397
  (10 shorter events, 0.2 us)
Async XLA Ops:
  0.6 7.0 %copy-start.3 = (f32[3,896]{1,0:T(4,128)S(1)}, f32[3,896]{1,0:T(4,128)}, u32[]{:S(2)}) copy-start(f32[3,896]{1,0:T(4,128)} %own.1) | copy-start | bytes 32260
  0.6 7.0 %copy-start.5 = (s32[2]{0:T(128)S(1)}, s32[2]{0:T(128)}, u32[]{:S(2)}) copy-start(s32[2]{0:T(128)} %dil.3) | copy-start | bytes 28
  0.7 7.0 %copy-start.4 = (f32[3,512]{1,0:T(4,128)S(1)}, f32[3,512]{1,0:T(4,128)}, u32[]{:S(2)}) copy-start(f32[3,512]{1,0:T(4,128)} %iw.1) | copy-start | bytes 18436
  0.7 7.0 %copy-start.2 = (f32[2,2,256]{2,1,0:T(2,128)S(1)}, f32[2,2,256]{2,1,0:T(2,128)}, u32[]{:S(2)}) copy-start(f32[2,2,256]{2,1,0:T(2,128)} %bias.3) | copy-start | bytes 12292
  0.7 7.0 %copy-start.1 = (bf16[2,256,512]{2,1,0:T(8,128)(2,1)S(1)}, bf16[2,256,512]{2,1,0:T(8,128)(2,1)}, u32[]{:S(2)}) copy-start(bf16[2,256,512]{2,1,0:T(8,128)(2,1)} %ow.5) | copy-start | bytes 1572868
  0.7 7.0 %copy-start.6 = (s32[3]{0:T(128)S(1)}, s32[3]{0:T(128)}, u32[]{:S(2)}) copy-start(s32[3]{0:T(128)} %offs.1) | copy-start | bytes 40
  0.7 6.9 %collective-permute-start = (f32[3,896]{1,0:T(4,128)}, f32[3,896]{1,0:T(4,128)S(1)}, u32[]{:S(2)}, u32[]{:S(2)}) collective-permute-start(f32[3,896]{1,0:T(4,128)} %own.1), channel_id=1, source_target_pairs={{0,2},{2,4},{4,6},{6,8},{8,10},{10,12},{12,14},{1,3},{3,5},{5,7},{... | collective-permute-start | bytes 32264 | tf_op jit(solution)/shard_map/ppermute | solution.py:312
  7.6 5.5 %copy-start = (bf16[896,512]{1,0:T(8,128)(2,1)S(1)}, bf16[896,512]{1,0:T(8,128)(2,1)}, u32[]{:S(2)}) copy-start(bf16[896,512]{1,0:T(8,128)(2,1)} %cot.5) | copy-start | bytes 2752516
  9.8 3.3 %collective-permute-start.1 = (bf16[1408,512]{1,0:T(8,128)(2,1)S(1)}, bf16[1408,512]{1,0:T(8,128)(2,1)S(1)}, u32[]{:S(2)}, u32[]{:S(2)}) collective-permute-start(bf16[1408,512]{1,0:T(8,128)(2,1)S(1)} %get-tuple-element.24.mine), channel_id=1, source_target_pairs={{0,1},{1,0},{2,3},{3,2},{4,5},{5,4},{6,7},{7,6},{8,9},{9,8},{10,11... | collective-permute-start | bytes 4325384 | tf_op jit(solution)/shard_map/ppermute | solution.py:26
  19.2 3.3 %collective-permute-start.2 = (bf16[1408,512]{1,0:T(8,128)(2,1)S(1)}, bf16[1408,512]{1,0:T(8,128)(2,1)S(1)}, u32[]{:S(2)}, u32[]{:S(2)}) collective-permute-start(bf16[1408,512]{1,0:T(8,128)(2,1)S(1)} %get-tuple-element.27.part), channel_id=1, source_target_pairs={{0,1},{1,0},{2,3},{3,2},{4,5},{5,4},{6,7},{7,6},{8,9},{9,8},{10,11... | collective-permute-start | bytes 4325384 | tf_op jit(solution)/shard_map/ppermute | solution.py:26
  26.4 38.0 %all-to-all-start = ((bf16[8,80,512]{2,1,0:T(8,128)(2,1)}), bf16[8,80,512]{2,1,0:T(8,128)(2,1)S(1)}, u32[]{:S(2)}, u32[]{:S(2)}) async-start(bf16[8,80,512]{2,1,0:T(8,128)(2,1)} %first_back.1), calls=%async_computation | async-start | bytes 1310720 | tf_op jit(solution)/shard_map/all_to_all | solution.py:276
  34.2 19.7 %collective-permute-start.4 = (bf16[4,128,512]{2,1,0:T(8,128)(2,1)S(1)}, bf16[4,128,512]{2,1,0:T(8,128)(2,1)S(1)}, u32[]{:S(2)}, u32[]{:S(2)}) collective-permute-start(bf16[4,128,512]{2,1,0:T(8,128)(2,1)S(1)} %get-tuple-element.38), channel_id=1, source_target_pairs={{0,2},{2,0},{4,6},{6,4},{8,10},{10,8},{12,14},{14,12},{1,3},{3,1},... | collective-permute-start | bytes 1572872 | tf_op jit(solution)/shard_map/ppermute | solution.py:268
  53.9 7.8 %collective-permute-start.5 = (bf16[2,128,512]{2,1,0:T(8,128)(2,1)S(1)}, bf16[2,128,512]{2,1,0:T(8,128)(2,1)S(1)}, u32[]{:S(2)}, u32[]{:S(2)}) collective-permute-start(bf16[2,128,512]{2,1,0:T(8,128)(2,1)S(1)} %get-tuple-element.40), channel_id=1, source_target_pairs={{0,4},{2,6},{4,0},{6,2},{8,12},{10,14},{12,8},{14,10},{1,5},{3,7},... | collective-permute-start | bytes 786440 | tf_op jit(solution)/shard_map/ppermute | solution.py:268
  61.7 8.1 %collective-permute-start.6 = (bf16[128,512]{1,0:T(8,128)(2,1)S(1)}, bf16[128,512]{1,0:T(8,128)(2,1)S(1)}, u32[]{:S(2)}, u32[]{:S(2)}) collective-permute-start(bf16[128,512]{1,0:T(8,128)(2,1)S(1)} %get-tuple-element.42), channel_id=1, source_target_pairs={{0,8},{2,10},{4,12},{6,14},{8,0},{10,2},{12,4},{14,6},{1,9},{3,11}... | collective-permute-start | bytes 393224 | tf_op jit(solution)/shard_map/ppermute | solution.py:268
  65.2 5.5 %collective-permute-start.3 = (f32[3,512]{1,0:T(4,128)S(1)}, f32[3,512]{1,0:T(4,128)S(1)}, u32[]{:S(2)}, u32[]{:S(2)}) collective-permute-start(f32[3,512]{1,0:T(4,128)S(1)} %slice.39), channel_id=1, source_target_pairs={{0,1},{1,0},{2,3},{3,2},{4,5},{5,4},{6,7},{7,6},{8,9},{9,8},{10,11... | collective-permute-start | bytes 18440 | tf_op jit(solution)/shard_map/ppermute | solution.py:26
  65.2 18.9 %all-to-all-start.1 = ((bf16[8,64,512]{2,1,0:T(8,128)(2,1)}), bf16[8,64,512]{2,1,0:T(8,128)(2,1)S(1)}, u32[]{:S(2)}, u32[]{:S(2)}) async-start(bf16[8,64,512]{2,1,0:T(8,128)(2,1)} %get-tuple-element.43), calls=%async_computation.1 | async-start | bytes 1048576 | tf_op jit(solution)/shard_map/all_to_all | solution.py:276

commit v3 on v2

--- a/solution.py
+++ b/solution.py
@@ -113,14 +113,9 @@
     d = dil[1]
     inside = jnp.where(lax.axis_index("seq") == 0, 0.0, 1.0)
 
-    def hidden(i, carry):
-        sl = pl.ds(pl.multiple_of(i * 128, 128), 128)
-        h = dot(st[sl, :], i3[...], ((1,), (0,)))
-        h = h + mine[sl, :].astype(F32) + other[sl, :].astype(F32)
-        h1[sl, :] = h * jnp.where(i * 128 < LAG, inside, 1.0)
-        return carry
-
-    lax.fori_loop(0, ext // 128, hidden, 0)
+    h1[...] = dot(st[...], i3[...], ((1,), (0,)))
+    h1[:LAG, :] = (h1[:LAG, :] + mine[:LAG, :].astype(F32) + other[:LAG, :].astype(F32)) * inside
+    h1[LAG:, :] = h1[LAG:, :] + mine[LAG:, :].astype(F32) + other[LAG:, :].astype(F32)
     near = LAG - pl.multiple_of((d // 8) * 8, 8)
 
     @pl.when(d >= 8)
@@ -129,7 +124,13 @@
 
     @pl.when(d < 8)
     def _():
-        joined[:, :channels] = pltpu.roll(h1[LAG - 8 :, :], d, 0)[8:].astype(BF16)
+        def step(i, carry):
+            at = pl.multiple_of(i * 64, 64)
+            x = h1[pl.ds(pl.multiple_of(LAG - 8 + at, 8), 72), :]
+            joined[pl.ds(at, 64), :channels] = pltpu.roll(x, d, 0)[8:].astype(BF16)
+            return carry
+
+        lax.fori_loop(0, rows // 64, step, 0)
 
     joined[:, channels:] = h1[LAG:, :].astype(BF16)
     for g in range(2):
@@ -149,21 +150,29 @@
         return total[0] + rows8(gf), total[1] + rows8(gs)
 
     zero = jnp.zeros((8, width), F32)
-    tf, ts = lax.fori_loop(0, rows // 32, local, (zero, zero))
+    tf, ts = lax.fori_loop(0, rows // 32, local, (zero, zero), unroll=4)
     bias1[:, :width] = jnp.sum(tf, axis=0, keepdims=True)
     bias1[:, width:] = jnp.sum(ts, axis=0, keepdims=True)
     acc[:LAG, :] = jnp.zeros((LAG, channels), F32)
     moved[:8, :] = jnp.zeros((8, channels), F32)
+    moved[rows + 8 :, :] = jnp.zeros((8, channels), F32)
     acc[LAG:, :] = untaps(gl1[...], w, 1, 1, channels)
-    moved[8:, :] = untaps(gl1[...], w, 1, 0, channels)
+    moved[8 : rows + 8, :] = untaps(gl1[...], w, 1, 0, channels)
 
     @pl.when(d >= 8)
     def _():
-        acc[pl.ds(pl.multiple_of(near, 8), rows), :] += moved[8:, :]
+        acc[pl.ds(pl.multiple_of(near, 8), rows), :] += moved[8 : rows + 8, :]
 
     @pl.when(d < 8)
     def _():
-        acc[LAG - 8 :, :] += pltpu.roll(moved[...], rows + 8 - d, 0)
+        def step(i, carry):
+            at = pl.multiple_of(i * 64, 64)
+            x = pltpu.roll(moved[pl.ds(at, 72), :], 72 - d, 0)[:64]
+            acc[pl.ds(pl.multiple_of(LAG - 8 + at, 8), 64), :] += x
+            return carry
+
+        lax.fori_loop(0, rows // 64, step, 0)
+        acc[ext - 8 :, :] += pltpu.roll(moved[rows:, :], 16 - d, 0)[:8]
 
     part[...] = acc[...].astype(BF16)
 
@@ -192,7 +201,7 @@
         return total[0] + rows8(gf), total[1] + rows8(gs)
 
     zero = jnp.zeros((8, width), F32)
-    tf, ts = lax.fori_loop(0, ext // 64, local, (zero, zero))
+    tf, ts = lax.fori_loop(0, ext // 64, local, (zero, zero), unroll=2)
     bias = jnp.concatenate([jnp.sum(tf, axis=0, keepdims=True), jnp.sum(ts, axis=0, keepdims=True)], axis=1)
     out_s[...] = dot(gate0[...], adj_s[...], ((0,), (0,))).reshape(out_s.shape)
     r2 = dot(srow[...], gl_s[...], ((1,), (0,)))
@@ -214,9 +223,11 @@
         outs[1][...] = small
     else:
         m = out_s.shape[1]
-        outs[0][:, :m, :] = out_s[...].astype(BF16)
-        outs[0][:, m : 2 * m, :] = do1[...].reshape(out_s.shape)
-        outs[0][:, 2 * m :, :] = jnp.broadcast_to(small.astype(BF16)[None], (8,) + small.shape)
+        z = lax.axis_index("seq") >> 1
+        for k in range(4):
+            outs[k][:m, :] = out_s[z ^ k].astype(BF16)
+            outs[k][m : 2 * m, :] = do1[pl.ds(pl.multiple_of((z ^ k) * m, m), m), :]
+            outs[k][2 * m :, :] = small.astype(BF16)
 
 
 def out_grad(scale, gate1, cot, out):
@@ -242,15 +253,37 @@
     send[...] = (keep[1] + got[1].astype(F32)).astype(BF16)
 
 
-def sum_blocks(got, blocks, small):
-    m = blocks.shape[1]
-    total = got[0].astype(F32)
-    for k in range(1, 8):
-        total = total + got[k].astype(F32)
+def quarter_sum(own, r1, r2, r3, total, held):
+    z = lax.axis_index("seq") >> 1
+    for k, ref in enumerate((own, r1, r2, r3)):
+        held[z ^ k] = ref[...].astype(F32)
+    total[...] = (held[0] + held[1] + held[2] + held[3]).astype(BF16)
+
+
+def half_sum(own, got, blocks, small):
+    m = blocks.shape[0]
+    total = own[...].astype(F32) + got[...].astype(F32)
+    blocks[...] = total[:m].astype(BF16)
     small[...] = total[m:]
-    both = total[:m].astype(BF16)
-    for k in range(8):
-        blocks[k] = both
+
+
+def first_conv(iw, small, out):
+    me = lax.axis_index("seq")
+    block, channels = out.shape[0], iw.shape[1]
+    at = pl.multiple_of((me & 3) * block, block)
+    i_hi, i_lo = halves(iw[:, pl.ds(at, block)])
+    r_hi, r_lo = halves(jnp.where(me < 4, small[:DET, :], small[DET : 2 * DET, :]))
+    left = jnp.concatenate([i_hi, i_lo, i_hi, jnp.zeros((7, block), F32)], axis=0).astype(BF16)
+    right = jnp.concatenate([r_hi, r_hi, r_lo, jnp.zeros((7, channels), F32)], axis=0).astype(BF16)
+    out[...] = dot(left, right, ((0,), (0,)))
+
+
+def finish(own, r1, r2, r3, out):
+    z = lax.axis_index("seq") >> 1
+    m = own.shape[0] // 2
+    for k, ref in enumerate((own, r1, r2, r3)):
+        for layer in range(2):
+            out[layer, pl.ds(pl.multiple_of((z ^ k) * m, m), m), :] = ref[layer * m : (layer + 1) * m, :].astype(F32)
 
 
 def scatter_sum(x, n):
@@ -285,7 +318,15 @@
     return pltpu.CompilerParams(vmem_limit_bytes=mib * 2**20)
 
 
-def call(kernel, out_shape, scratch=()):
+def after(x, y):
+    return lax.optimization_barrier((x, y))[0]
+
+
+def cost(us):
+    return pl.CostEstimate(flops=int(us * 8e8), bytes_accessed=int(us * 3e6), transcendentals=0)
+
+
+def call(kernel, out_shape, scratch=(), us=1.0):
     def run(*args):
         count = len(out_shape) if isinstance(out_shape, list) else 0
         return pl.pallas_call(
@@ -295,6 +336,7 @@
             out_specs=[VMEM] * count if count else VMEM,
             scratch_shapes=list(scratch),
             compiler_params=limit(8),
+            cost_estimate=cost(us),
             name=getattr(kernel, "func", kernel).__name__,
         )(*args)
 
@@ -327,6 +369,7 @@
         out_specs=[VMEM] * 7,
         scratch_shapes=[pltpu.VMEM((8, full), F32), pltpu.VMEM((8, ext), F32)],
         compiler_params=limit(10),
+        cost_estimate=cost(2),
         name="first_layer",
     )(offsets, dilation, prev, strain, input_weight, weight, conv_bias, out_weight)
     other = swap(mine)
@@ -344,11 +387,12 @@
         scratch_shapes=[
             pltpu.VMEM((ext, channels), F32),
             pltpu.VMEM((ext, channels), F32),
-            pltpu.VMEM((rows + 8, channels), F32),
+            pltpu.VMEM((rows + 16, channels), F32),
             pltpu.VMEM((rows, 2 * width), F32),
             pltpu.VMEM((rows, width), F32),
         ],
         compiler_params=limit(28),
+        cost_estimate=cost(7),
         name="second_layer",
     )(dilation, mine, other, st, i3, weight, conv_bias, out_weight, cotangent)
     apart = swap(part)
@@ -358,13 +402,16 @@
             conv_grad,
             [shape((4, channels // 4, 2 * width), F32), shape((4, channels // 4, 2 * width), BF16)],
             [pltpu.VMEM((8, channels // 4, 2 * width), F32)],
+            1.5,
         )(joined, gl1)
         c_got = along(c_send, 1)
+        apart = after(apart, c_send)
     do1 = call(functools.partial(out_grad, scale), shape((width, channels), BF16))(gate1, cotangent)
     m = width // n
     if n == 8:
-        back_shapes = [shape((n, 2 * m + 16, channels), BF16)]
-        held = (n, m, channels)
+        m = width // 4
+        back_shapes = [shape((2 * m + 16, channels), BF16)] * 4
+        held = (4, m, channels)
     else:
         back_shapes = [shape((width, channels), F32), shape((16, 2 * width), F32)]
         held = (width, channels)
@@ -380,21 +427,22 @@
             pltpu.VMEM((ext, width), F32),
         ],
         compiler_params=limit(16),
+        cost_estimate=cost(4),
         name="first_back",
     )(part, apart, cotangent, gate0, fa, fb, srow, out_weight, weight, bias1, do1)
     if n == 8:
-        back_got = all_to_all(back[0])
+        got = [along(back[k], 2 * k) for k in (1, 2, 3)]
+        c_keep = after(c_keep, back[0])
         c_two, c_send = call(pair_add, pair_shapes(2, channels // 4, 2 * width))(c_keep, c_got)
         c_got = along(c_send, 2)
-        blocks, small = call(
-            sum_blocks, [shape((n, 2 * m, channels), BF16), shape((16, channels), F32)]
-        )(back_got)
-        do = all_to_all(blocks)
+        quarter = call(quarter_sum, shape(back[0].shape, BF16), [pltpu.VMEM((4,) + back[0].shape, F32)])(back[0], *got)
+        other = along(quarter, 1)
         c_own, c_send = call(pair_add_again, pair_shapes(0, channels // 4, 2 * width))(c_two, c_got)
         c_got = along(c_send, 4)
+        blocks, small = call(half_sum, [shape((2 * m, channels), BF16), shape((16, channels), F32)])(quarter, other)
+        got = [along(blocks, 2 * k) for k in (1, 2, 3)]
         dw1 = c_own + c_got.astype(F32)
-        do = jnp.transpose(do.reshape(n, 2, m, channels), (1, 0, 2, 3)).astype(F32)
-        grad_out = do.reshape(2, width, channels)
+        grad_out = call(finish, shape((2, width, channels), F32))(blocks, *got)
     else:
         dw1 = scatter_sum(dot(joined, gl1, ((0,), (0,))), n)
         do1 = scatter_sum(do1, n)
@@ -406,9 +454,12 @@
     grad_input = g + swap(g)
     grad_bias = bias.reshape(2, 2, width)
     block = 2 * channels // n
-    mine_iw = lax.dynamic_slice_in_dim(input_weight, (me * block) % channels, block, 1)
-    mine_r = jnp.where(me * block < channels, r[:DET], r[DET:])
-    dw0 = sum(mine_iw[k][:, None] * mine_r[k][None, :] for k in range(DET))
+    if n == 8:
+        dw0 = call(first_conv, shape((block, 2 * width), F32))(input_weight, small)
+    else:
+        mine_iw = lax.dynamic_slice_in_dim(input_weight, (me * block) % channels, block, 1)
+        mine_r = jnp.where(me * block < channels, r[:DET], r[DET:])
+        dw0 = sum(mine_iw[k][:, None] * mine_r[k][None, :] for k in range(DET))
     grad_conv = jnp.stack([dw0, dw1]).reshape(2, block, 2, width)
     return (grad_input, grad_conv, grad_bias, grad_out)
 

time: 86.6 us -> 67.1 us (0.77); the launches traced: 85.2 us -> 66.9 us
  waiting for transfers between devices: 41.9 us -> 27.2 us
  Pallas kernels: 15.1 us -> 13.8 us
  local copies, waits for them, and re-layouts: 3.83 us -> 2.85 us
    all_to_all x2 -> x0, waiting for transfers between devices: 11.2 us -> none  [all_to_all(): return lax.all_to_all(x, 'seq', 0, 0, tiled=True)]
    all_to_all x2 -> x0, starting transfers between devices: 9.82 us -> none  [all_to_all(): return lax.all_to_all(x, 'seq', 0, 0, tiled=True)]
    ppermute x3 -> x10, starting transfers between devices: 6.21 us -> 15.3 us  [along(): return lax.ppermute(x, 'seq', [(i, i ^ k) for i in range(n)])]
    ppermute x3, waiting for transfers between devices: 5.83 us -> 3.36 us  [swap(): return lax.ppermute(x, 'tensor', [(0, 1), (1, 0)])]
    pallas_call x1, Pallas kernels: 6.18 us -> 5.11 us  [body(): pl.pallas_call(functools.partial(second_layer, scale), out_shape=[shape((...]
    reshape x1 -> x0, local copies, waits for them, and re-layouts: 1.07 us -> none  [body(): grad_out = do.reshape(2, width, channels)]
    ppermute x3 -> x10, waiting for transfers between devices: 24.9 us -> 23.9 us  [along(): return lax.ppermute(x, 'seq', [(i, i ^ k) for i in range(n)])]
    pallas_call x5 -> x8, Pallas kernels: 2.95 us -> 3.59 us  [run(): pl.pallas_call(kernel, out_shape=out_shape, in_specs=[VMEM] * len(args),...]
  transfers between devices with their start and end apart: 9 -> 14, of which waited for: 6 -> 8; matrix products, arithmetic and copies ran while one was open for 6% -> 7% of each run, Pallas kernels for 3% -> 8%
where the time goes in v3:
time: 67.1 us; the launch traced here: 66.9 us
  waiting for transfers between devices  27.2 us (41%)
  starting transfers between devices  20.5 us (31%)
  Pallas kernels  13.8 us (21%)
  local copies, waits for them, and re-layouts  2.85 us (4%)
  other arithmetic  1.67 us (2%)
  between operations  0.87 us (1%)
    ppermute x10, waiting for transfers between devices, along(): return lax.ppermute(x, 'seq', [(i, i ^ k) for i in range(n)])  23.9 us
    ppermute x10, starting transfers between devices, along(): return lax.ppermute(x, 'seq', [(i, i ^ k) for i in range(n)])  15.3 us
    pallas_call x1, Pallas kernels, body(): pl.pallas_call(functools.partial(second_layer, scale), out_shape=[shape((...  5.11 us
    ppermute x1, starting transfers between devices, body(): prev = lax.ppermute(strain, 'seq', [(i, i + 1) for i in range(n - 1)])  5 us
    pallas_call x8, Pallas kernels, run(): pl.pallas_call(kernel, out_shape=out_shape, in_specs=[VMEM] * len(args),...  3.59 us
    ppermute x3, waiting for transfers between devices, swap(): return lax.ppermute(x, 'tensor', [(0, 1), (1, 0)])  3.36 us
    pallas_call x1, Pallas kernels, body(): pl.pallas_call(functools.partial(first_back, scale), out_shape=back_shape...  2.98 us
    pallas_call x1, Pallas kernels, body(): pl.pallas_call(first_layer, out_shape=[shape((ext, channels), BF16), shap...  2.09 us
  transfers between devices with their start and end apart: 14, of which 8 were waited for; matrix products, arithmetic and copies ran while one was open for 7% of the time, Pallas kernels for 8%

profile of v3, /device:TPU:0, one launch (start us, length us, event | category | flops | bytes accessed | tf_op | source)
XLA Modules:
  0.0 66.9 jit_solution(481956760100981266)
XLA Ops:
  0.6 0.0 copy-start.2
  0.6 0.0 copy-start.1
  0.7 0.0 copy-start.4
  0.7 0.0 copy-start.3
  0.7 0.0 copy-start.6
  0.7 0.0 copy-start.5
  0.7 5.0 %collective-permute-start = (f32[3,896]{1,0:T(4,128)}, f32[3,896]{1,0:T(4,128)S(1)}, u32[]{:S(2)}, u32[]{:S(2)}) collective-permute-start(f32[3,896]{1,0:T(4,128)} %own.1), channel_id=1, source_target_pairs={{0,2},{2,4},{4,6},{6,8},{8,10},{10,12},{12,14},{1,3},{3,5},{5,7},{... | collective-permute-start | bytes 32264 | tf_op jit(solution)/shard_map/ppermute | solution.py:354
  5.7 1.9 %copy.14 = bf16[2,1024,2,256]{3,1,2,0:T(8,128)(2,1)S(1)} copy(bf16[2,1024,2,256]{3,2,1,0:T(2,128)(2,1)} %param.12) | data formatting | bytes 4194304 | tf_op args[4]
  7.6 0.0 collective-permute-done.prev
  7.6 0.0 copy-done.2
  7.6 0.0 copy-done.1
  7.6 0.0 copy-done.4
  7.6 0.0 copy-done.3
  7.6 0.0 copy-done.6
  7.6 0.0 copy-done.5
  7.6 0.0 copy-start
  7.7 2.1 %first_layer.1 = (bf16[1408,512]{1,0:T(8,128)(2,1)S(1)}, bf16[1408,256]{1,0:T(8,128)(2,1)S(1)}, f32[1408,256]{1,0:T(8,128)S(1)}, f32[1408,256]{1,0:T(8,128)S(1)}...) custom-call(s32[3]{0:T(128)S(1)} %copy-done.5, s32[2]{0:T(128)S(1)} %copy-done.6, ...), custom_call_target="tpu_custom_call" | custom-call | flops 1600000000 | bytes 6000000 | tf_op jit(solution)/shard_map/first_layer/pallas_call | solution.py:357
  9.8 0.1 collective-permute-start.1
  9.8 3.2 %collective-permute-done.1.other = bf16[1408,512]{1,0:T(8,128)(2,1)S(1)} collective-permute-done((bf16[1408,512]{1,0:T(8,128)(2,1)S(1)}, bf16[1408,512]{1,0:T(8,128)(2,1)S(1)}, u32[]{:S(2)}, u32[]{:S(2)}) %collective-permute-start.1) | collective-permute-done | bytes 1441824 | tf_op jit(solution)/shard_map/ppermute | solution.py:26
  13.0 0.0 copy-done
  13.0 5.1 %second_layer.1 = (bf16[1408,512]{1,0:T(8,128)(2,1)S(1)}, bf16[896,512]{1,0:T(8,128)(2,1)S(1)}, bf16[896,256]{1,0:T(8,128)(2,1)S(1)}, bf16[896,1024]{1,0:T(8,128)(2,1)S(1)}, f32[1,512]{1,0:T(1,128)S(1)}) custom-call(s32[2]{0:T(128)S(1)} %copy-done.6, bf16[1408,512]{1,0:T(8,128)(2,1)S(1)} %get-tuple-element.30.mine, ...), custom_call_target="tpu_custom_call" | custom-call | flops 5600000000 | bytes 21000000 | tf_op jit(solution)/shard_map/second_layer/pallas_call | solution.py:376
  18.2 0.2 collective-permute-start.2
  18.4 1.5 %conv_grad.1 = (f32[4,128,512]{2,1,0:T(8,128)S(1)}, bf16[4,128,512]{2,1,0:T(8,128)(2,1)S(1)}) custom-call(bf16[896,1024]{1,0:T(8,128)(2,1)S(1)} %get-tuple-element.34.joined, bf16[896,512]{1,0:T(8,128)(2,1)S(1)} %get-tuple-element.35.gl1), custom_call_target="tpu_custom_call" | custom-call | flops 1200000000 | bytes 4500000 | tf_op jit(solution)/shard_map/conv_grad/pallas_call | solution.py:332
  19.9 2.1 %collective-permute-start.8 = (bf16[4,128,512]{2,1,0:T(8,128)(2,1)S(1)}, bf16[4,128,512]{2,1,0:T(8,128)(2,1)S(1)}, u32[]{:S(2)}, u32[]{:S(2)}) collective-permute-start(bf16[4,128,512]{2,1,0:T(8,128)(2,1)S(1)} %get-tuple-element.36), channel_id=1, source_target_pairs={{0,2},{2,0},{4,6},{6,4},{8,10},{10,8},{12,14},{14,12},{1,3},{3,1},... | collective-permute-start | bytes 1572872 | tf_op jit(solution)/shard_map/ppermute | solution.py:301
  21.9 0.5 out_grad.1.do1
  22.4 0.0 collective-permute-done.2.apart
  22.4 3.0 %first_back.1 = (bf16[144,512]{1,0:T(8,128)(2,1)S(1)}, bf16[144,512]{1,0:T(8,128)(2,1)S(1)}, bf16[144,512]{1,0:T(8,128)(2,1)S(1)}, bf16[144,512]{1,0:T(8,128)(2,1)S(1)}) custom-call(bf16[1408,512]{1,0:T(8,128)(2,1)S(1)} %get-tuple-element.33.part, bf16[1408,512]{1,0:T(8,128)(2,1)S(1)} %collective-permute-done.2.apart, bf16[896,512]{1,0:T(8,128)(2,1)S(1)} %copy-done, ...), custom_call_target="tpu_custom_call" | custom-call | flops 3200000000 | bytes 12000000 | tf_op jit(solution)/shard_map/first_back/pallas_call | solution.py:418
  25.4 2.1 %collective-permute-start.3 = (bf16[144,512]{1,0:T(8,128)(2,1)S(1)}, bf16[144,512]{1,0:T(8,128)(2,1)S(1)}, u32[]{:S(2)}, u32[]{:S(2)}) collective-permute-start(bf16[144,512]{1,0:T(8,128)(2,1)S(1)} %get-tuple-element.45), channel_id=1, source_target_pairs={{0,4},{2,6},{4,0},{6,2},{8,12},{10,14},{12,8},{14,10},{1,5},{3,7},... | collective-permute-start | bytes 442376 | tf_op jit(solution)/shard_map/ppermute | solution.py:301
  27.5 2.6 %collective-permute-start.4 = (bf16[144,512]{1,0:T(8,128)(2,1)S(1)}, bf16[144,512]{1,0:T(8,128)(2,1)S(1)}, u32[]{:S(2)}, u32[]{:S(2)}) collective-permute-start(bf16[144,512]{1,0:T(8,128)(2,1)S(1)} %get-tuple-element.46), channel_id=1, source_target_pairs={{0,8},{2,10},{4,12},{6,14},{8,0},{10,2},{12,4},{14,6},{1,9},{3,11}... | collective-permute-start | bytes 442376 | tf_op jit(solution)/shard_map/ppermute | solution.py:301
  30.1 0.0 collective-permute-start.5
  30.1 4.3 %collective-permute-done.8.got = bf16[4,128,512]{2,1,0:T(8,128)(2,1)S(1)} collective-permute-done((bf16[4,128,512]{2,1,0:T(8,128)(2,1)S(1)}, bf16[4,128,512]{2,1,0:T(8,128)(2,1)S(1)}, u32[]{:S(2)}, u32[]{:S(2)}) %collective-permute-start.8) | collective-permute-done | bytes 524320 | tf_op jit(solution)/shard_map/ppermute | solution.py:301
  34.4 0.1 pair_add.1
  34.5 2.8 %collective-permute-start.9 = (bf16[2,128,512]{2,1,0:T(8,128)(2,1)S(1)}, bf16[2,128,512]{2,1,0:T(8,128)(2,1)S(1)}, u32[]{:S(2)}, u32[]{:S(2)}) collective-permute-start(bf16[2,128,512]{2,1,0:T(8,128)(2,1)S(1)} %get-tuple-element.52), channel_id=1, source_target_pairs={{0,4},{2,6},{4,0},{6,2},{8,12},{10,14},{12,8},{14,10},{1,5},{3,7},... | collective-permute-start | bytes 786440 | tf_op jit(solution)/shard_map/ppermute | solution.py:301
  37.3 0.0 collective-permute-done.3.r1
  37.3 4.1 %collective-permute-done.4.r2 = bf16[144,512]{1,0:T(8,128)(2,1)S(1)} collective-permute-done((bf16[144,512]{1,0:T(8,128)(2,1)S(1)}, bf16[144,512]{1,0:T(8,128)(2,1)S(1)}, u32[]{:S(2)}, u32[]{:S(2)}) %collective-permute-start.4) | collective-permute-done | bytes 147488 | tf_op jit(solution)/shard_map/ppermute | solution.py:301
  41.5 0.0 collective-permute-done.5.r3
  41.5 0.2 quarter_sum.1.own
  41.6 1.1 %collective-permute-start.6 = (bf16[144,512]{1,0:T(8,128)(2,1)S(1)}, bf16[144,512]{1,0:T(8,128)(2,1)S(1)}, u32[]{:S(2)}, u32[]{:S(2)}) collective-permute-start(bf16[144,512]{1,0:T(8,128)(2,1)S(1)} %quarter_sum.1.own), channel_id=1, source_target_pairs={{0,2},{2,0},{4,6},{6,4},{8,10},{10,8},{12,14},{14,12},{1,3},{3,1},... | collective-permute-start | bytes 442376 | tf_op jit(solution)/shard_map/ppermute | solution.py:301
  42.7 3.7 %collective-permute-done.9.got = bf16[2,128,512]{2,1,0:T(8,128)(2,1)S(1)} collective-permute-done((bf16[2,128,512]{2,1,0:T(8,128)(2,1)S(1)}, bf16[2,128,512]{2,1,0:T(8,128)(2,1)S(1)}, u32[]{:S(2)}, u32[]{:S(2)}) %collective-permute-start.9) | collective-permute-done | bytes 262176 | tf_op jit(solution)/shard_map/ppermute | solution.py:301
  46.4 0.3 collective-permute-start.10
  46.6 0.2 collective-permute-done.6.got
  46.9 2.5 %collective-permute-start.13 = (bf16[128,512]{1,0:T(8,128)(2,1)S(1)}, bf16[128,512]{1,0:T(8,128)(2,1)S(1)}, u32[]{:S(2)}, u32[]{:S(2)}) collective-permute-start(bf16[128,512]{1,0:T(8,128)(2,1)S(1)} %get-tuple-element.55.own), channel_id=1, source_target_pairs={{0,12},{2,14},{4,8},{6,10},{8,4},{10,6},{12,0},{14,2},{1,13},{3,15... | collective-permute-start | bytes 393224 | tf_op jit(solution)/shard_map/ppermute | solution.py:301
  49.3 1.7 %collective-permute-start.12 = (bf16[128,512]{1,0:T(8,128)(2,1)S(1)}, bf16[128,512]{1,0:T(8,128)(2,1)S(1)}, u32[]{:S(2)}, u32[]{:S(2)}) collective-permute-start(bf16[128,512]{1,0:T(8,128)(2,1)S(1)} %get-tuple-element.55.own), channel_id=1, source_target_pairs={{0,8},{2,10},{4,12},{6,14},{8,0},{10,2},{12,4},{14,6},{1,9},{3,11}... | collective-permute-start | bytes 393224 | tf_op jit(solution)/shard_map/ppermute | solution.py:301
  51.1 0.3 collective-permute-start.11
  51.3 0.0 collective-permute-start.7
  51.3 0.2 first_conv.1
  51.6 0.6 reshape.16
  52.2 0.2 stack.9
  52.4 0.1 collective-permute-done.7
  52.5 0.6 slice_add_fusion
  53.1 7.2 %collective-permute-done.10 = bf16[128,512]{1,0:T(8,128)(2,1)S(1)} collective-permute-done((bf16[128,512]{1,0:T(8,128)(2,1)S(1)}, bf16[128,512]{1,0:T(8,128)(2,1)S(1)}, u32[]{:S(2)}, u32[]{:S(2)}) %collective-permute-start.10) | collective-permute-done | bytes 131104 | tf_op jit(solution)/shard_map/ppermute | solution.py:301
  60.4 0.2 stack.10
  60.6 1.0 %pad_maximum_fusion = f32[2,128,2,256]{3,2,1,0:T(2,128)} fusion(f32[1,128,2,256]{3,2,1,0:T(2,128)S(1)} %stack.10, f32[1,128,2,256]{3,2,1,0:T(2,128)S(1)} %stack.9), kind=kLoop, calls=%fused_computation.1 | loop fusion | flops 131072 | bytes 1048576 | tf_op jit(solution)/shard_map/stack | solution.py:463
  61.6 0.0 collective-permute-done.13.r3
  61.6 4.3 %collective-permute-done.12.r2 = bf16[128,512]{1,0:T(8,128)(2,1)S(1)} collective-permute-done((bf16[128,512]{1,0:T(8,128)(2,1)S(1)}, bf16[128,512]{1,0:T(8,128)(2,1)S(1)}, u32[]{:S(2)}, u32[]{:S(2)}) %collective-permute-start.12) | collective-permute-done | bytes 131104 | tf_op jit(solution)/shard_map/ppermute | solution.py:301
  65.9 0.0 collective-permute-done.11.r1
  65.9 1.0 %finish.1 = f32[2,256,512]{2,1,0:T(8,128)} custom-call(bf16[128,512]{1,0:T(8,128)(2,1)S(1)} %get-tuple-element.55.own, bf16[128,512]{1,0:T(8,128)(2,1)S(1)} %collective-permute-done.11.r1, bf16[128,512]{1,0:T(8,128)(2,1)S(1)} %collective-permute-done.12.r2, bf16[128,512]{1,0:T(8,128)(2,1)S(1)} %collective-permute-done.13.r3), custom_call_target="tpu_custom_call" | custom-call | flops 800000000 | bytes 3000000 | tf_op jit(solution)/shard_map/finish/pallas_call | solution.py:332
  (5 shorter events, 0.1 us)
Async XLA Ops:
  0.6 7.0 %copy-start.2 = (f32[3,896]{1,0:T(4,128)S(1)}, f32[3,896]{1,0:T(4,128)}, u32[]{:S(2)}) copy-start(f32[3,896]{1,0:T(4,128)} %own.1) | copy-start | bytes 32260
  0.6 7.0 %copy-start.1 = (bf16[2,256,512]{2,1,0:T(8,128)(2,1)S(1)}, bf16[2,256,512]{2,1,0:T(8,128)(2,1)}, u32[]{:S(2)}) copy-start(bf16[2,256,512]{2,1,0:T(8,128)(2,1)} %ow.5) | copy-start | bytes 1572868
  0.7 7.0 %copy-start.4 = (f32[2,2,256]{2,1,0:T(2,128)S(1)}, f32[2,2,256]{2,1,0:T(2,128)}, u32[]{:S(2)}) copy-start(f32[2,2,256]{2,1,0:T(2,128)} %bias.3) | copy-start | bytes 12292
  0.7 7.0 %copy-start.3 = (f32[3,512]{1,0:T(4,128)S(1)}, f32[3,512]{1,0:T(4,128)}, u32[]{:S(2)}) copy-start(f32[3,512]{1,0:T(4,128)} %iw.3) | copy-start | bytes 18436
  0.7 7.0 %copy-start.6 = (s32[2]{0:T(128)S(1)}, s32[2]{0:T(128)}, u32[]{:S(2)}) copy-start(s32[2]{0:T(128)} %dil.3) | copy-start | bytes 28
  0.7 7.0 %copy-start.5 = (s32[3]{0:T(128)S(1)}, s32[3]{0:T(128)}, u32[]{:S(2)}) copy-start(s32[3]{0:T(128)} %offs.1) | copy-start | bytes 40
  0.7 6.9 %collective-permute-start = (f32[3,896]{1,0:T(4,128)}, f32[3,896]{1,0:T(4,128)S(1)}, u32[]{:S(2)}, u32[]{:S(2)}) collective-permute-start(f32[3,896]{1,0:T(4,128)} %own.1), channel_id=1, source_target_pairs={{0,2},{2,4},{4,6},{6,8},{8,10},{10,12},{12,14},{1,3},{3,5},{5,7},{... | collective-permute-start | bytes 32264 | tf_op jit(solution)/shard_map/ppermute | solution.py:354
  7.6 5.4 %copy-start = (bf16[896,512]{1,0:T(8,128)(2,1)S(1)}, bf16[896,512]{1,0:T(8,128)(2,1)}, u32[]{:S(2)}) copy-start(bf16[896,512]{1,0:T(8,128)(2,1)} %cot.5) | copy-start | bytes 2752516
  9.8 3.3 %collective-permute-start.1 = (bf16[1408,512]{1,0:T(8,128)(2,1)S(1)}, bf16[1408,512]{1,0:T(8,128)(2,1)S(1)}, u32[]{:S(2)}, u32[]{:S(2)}) collective-permute-start(bf16[1408,512]{1,0:T(8,128)(2,1)S(1)} %get-tuple-element.30.mine), channel_id=1, source_target_pairs={{0,1},{1,0},{2,3},{3,2},{4,5},{5,4},{6,7},{7,6},{8,9},{9,8},{10,11... | collective-permute-start | bytes 4325384 | tf_op jit(solution)/shard_map/ppermute | solution.py:26
  18.2 4.3 %collective-permute-start.2 = (bf16[1408,512]{1,0:T(8,128)(2,1)S(1)}, bf16[1408,512]{1,0:T(8,128)(2,1)S(1)}, u32[]{:S(2)}, u32[]{:S(2)}) collective-permute-start(bf16[1408,512]{1,0:T(8,128)(2,1)S(1)} %get-tuple-element.33.part), channel_id=1, source_target_pairs={{0,1},{1,0},{2,3},{3,2},{4,5},{5,4},{6,7},{7,6},{8,9},{9,8},{10,11... | collective-permute-start | bytes 4325384 | tf_op jit(solution)/shard_map/ppermute | solution.py:26
  19.9 14.5 %collective-permute-start.8 = (bf16[4,128,512]{2,1,0:T(8,128)(2,1)S(1)}, bf16[4,128,512]{2,1,0:T(8,128)(2,1)S(1)}, u32[]{:S(2)}, u32[]{:S(2)}) collective-permute-start(bf16[4,128,512]{2,1,0:T(8,128)(2,1)S(1)} %get-tuple-element.36), channel_id=1, source_target_pairs={{0,2},{2,0},{4,6},{6,4},{8,10},{10,8},{12,14},{14,12},{1,3},{3,1},... | collective-permute-start | bytes 1572872 | tf_op jit(solution)/shard_map/ppermute | solution.py:301
  25.4 11.9 %collective-permute-start.3 = (bf16[144,512]{1,0:T(8,128)(2,1)S(1)}, bf16[144,512]{1,0:T(8,128)(2,1)S(1)}, u32[]{:S(2)}, u32[]{:S(2)}) collective-permute-start(bf16[144,512]{1,0:T(8,128)(2,1)S(1)} %get-tuple-element.45), channel_id=1, source_target_pairs={{0,4},{2,6},{4,0},{6,2},{8,12},{10,14},{12,8},{14,10},{1,5},{3,7},... | collective-permute-start | bytes 442376 | tf_op jit(solution)/shard_map/ppermute | solution.py:301
  27.5 14.0 %collective-permute-start.4 = (bf16[144,512]{1,0:T(8,128)(2,1)S(1)}, bf16[144,512]{1,0:T(8,128)(2,1)S(1)}, u32[]{:S(2)}, u32[]{:S(2)}) collective-permute-start(bf16[144,512]{1,0:T(8,128)(2,1)S(1)} %get-tuple-element.46), channel_id=1, source_target_pairs={{0,8},{2,10},{4,12},{6,14},{8,0},{10,2},{12,4},{14,6},{1,9},{3,11}... | collective-permute-start | bytes 442376 | tf_op jit(solution)/shard_map/ppermute | solution.py:301
  30.1 11.4 %collective-permute-start.5 = (bf16[144,512]{1,0:T(8,128)(2,1)S(1)}, bf16[144,512]{1,0:T(8,128)(2,1)S(1)}, u32[]{:S(2)}, u32[]{:S(2)}) collective-permute-start(bf16[144,512]{1,0:T(8,128)(2,1)S(1)} %get-tuple-element.47), channel_id=1, source_target_pairs={{0,12},{2,14},{4,8},{6,10},{8,4},{10,6},{12,0},{14,2},{1,13},{3,15... | collective-permute-start | bytes 442376 | tf_op jit(solution)/shard_map/ppermute | solution.py:301
  34.5 11.8 %collective-permute-start.9 = (bf16[2,128,512]{2,1,0:T(8,128)(2,1)S(1)}, bf16[2,128,512]{2,1,0:T(8,128)(2,1)S(1)}, u32[]{:S(2)}, u32[]{:S(2)}) collective-permute-start(bf16[2,128,512]{2,1,0:T(8,128)(2,1)S(1)} %get-tuple-element.52), channel_id=1, source_target_pairs={{0,4},{2,6},{4,0},{6,2},{8,12},{10,14},{12,8},{14,10},{1,5},{3,7},... | collective-permute-start | bytes 786440 | tf_op jit(solution)/shard_map/ppermute | solution.py:301
  41.6 5.2 %collective-permute-start.6 = (bf16[144,512]{1,0:T(8,128)(2,1)S(1)}, bf16[144,512]{1,0:T(8,128)(2,1)S(1)}, u32[]{:S(2)}, u32[]{:S(2)}) collective-permute-start(bf16[144,512]{1,0:T(8,128)(2,1)S(1)} %quarter_sum.1.own), channel_id=1, source_target_pairs={{0,2},{2,0},{4,6},{6,4},{8,10},{10,8},{12,14},{14,12},{1,3},{3,1},... | collective-permute-start | bytes 442376 | tf_op jit(solution)/shard_map/ppermute | solution.py:301
  46.4 14.0 %collective-permute-start.10 = (bf16[128,512]{1,0:T(8,128)(2,1)S(1)}, bf16[128,512]{1,0:T(8,128)(2,1)S(1)}, u32[]{:S(2)}, u32[]{:S(2)}) collective-permute-start(bf16[128,512]{1,0:T(8,128)(2,1)S(1)} %get-tuple-element.54), channel_id=1, source_target_pairs={{0,8},{2,10},{4,12},{6,14},{8,0},{10,2},{12,4},{14,6},{1,9},{3,11}... | collective-permute-start | bytes 393224 | tf_op jit(solution)/shard_map/ppermute | solution.py:301
  46.9 14.7 %collective-permute-start.13 = (bf16[128,512]{1,0:T(8,128)(2,1)S(1)}, bf16[128,512]{1,0:T(8,128)(2,1)S(1)}, u32[]{:S(2)}, u32[]{:S(2)}) collective-permute-start(bf16[128,512]{1,0:T(8,128)(2,1)S(1)} %get-tuple-element.55.own), channel_id=1, source_target_pairs={{0,12},{2,14},{4,8},{6,10},{8,4},{10,6},{12,0},{14,2},{1,13},{3,15... | collective-permute-start | bytes 393224 | tf_op jit(solution)/shard_map/ppermute | solution.py:301
  49.3 16.5 %collective-permute-start.12 = (bf16[128,512]{1,0:T(8,128)(2,1)S(1)}, bf16[128,512]{1,0:T(8,128)(2,1)S(1)}, u32[]{:S(2)}, u32[]{:S(2)}) collective-permute-start(bf16[128,512]{1,0:T(8,128)(2,1)S(1)} %get-tuple-element.55.own), channel_id=1, source_target_pairs={{0,8},{2,10},{4,12},{6,14},{8,0},{10,2},{12,4},{14,6},{1,9},{3,11}... | collective-permute-start | bytes 393224 | tf_op jit(solution)/shard_map/ppermute | solution.py:301
  51.1 14.8 %collective-permute-start.11 = (bf16[128,512]{1,0:T(8,128)(2,1)S(1)}, bf16[128,512]{1,0:T(8,128)(2,1)S(1)}, u32[]{:S(2)}, u32[]{:S(2)}) collective-permute-start(bf16[128,512]{1,0:T(8,128)(2,1)S(1)} %get-tuple-element.55.own), channel_id=1, source_target_pairs={{0,4},{2,6},{4,0},{6,2},{8,12},{10,14},{12,8},{14,10},{1,5},{3,7},... | collective-permute-start | bytes 393224 | tf_op jit(solution)/shard_map/ppermute | solution.py:301
  51.3 1.2 %collective-permute-start.7 = (f32[3,512]{1,0:T(4,128)S(1)}, f32[3,512]{1,0:T(4,128)S(1)}, u32[]{:S(2)}, u32[]{:S(2)}) collective-permute-start(f32[3,512]{1,0:T(4,128)S(1)} %slice.6), channel_id=1, source_target_pairs={{0,1},{1,0},{2,3},{3,2},{4,5},{5,4},{6,7},{7,6},{8,9},{9,8},{10,11... | collective-permute-start | bytes 18440 | tf_op jit(solution)/shard_map/ppermute | solution.py:26

commit v4 on v3

--- a/solution.py
+++ b/solution.py
@@ -56,10 +56,10 @@
     return [(0, LAG)] + [(at, min(512, ext - at)) for at in range(LAG, ext, 512)]
 
 
-def first_layer(offs, dil, prev, own, iw, w, bias, ow, mine, gate0, fa, fb, st, srow, i3, line, sig):
+def first_layer(offs, dil, prev, own, iw, w, bias, gate0, fa, fb, st, srow, i3, line, sig):
     rows = own.shape[1]
     channels = iw.shape[1]
-    width = ow.shape[1]
+    width = w.shape[3]
     ext = rows + LAG
     full = line.shape[1]
     spare = full - 2 * rows
@@ -99,23 +99,25 @@
         gate = th * sg
         fa[sl, :] = sg - gate * th
         fb[sl, :] = gate - gate * sg
-        gate = gate.astype(BF16)
-        gate0[sl, :] = gate
-        mine[sl, :] = dot(gate, ow[0], ((1,), (0,))).astype(BF16)
+        gate0[sl, :] = gate.astype(BF16)
+
+
+def own_mix(scale, st, i3, gate0, ow, cot, hm, gg):
+    hm[...] = dot(st[...], i3[...], ((1,), (0,))) + dot(gate0[...], ow[0], ((1,), (0,)))
+    gg[...] = dot(cot[...], ow[1], ((1,), (1,))) * scale
 
 
 def second_layer(
-    scale, dil, mine, other, st, i3, w, bias, ow, cot, part, gl1, gate1, joined, bias1, h1, acc, moved, pre, gg
+    dil, hm, gg, gate_far, ow_far, w, bias, part, gl1, gate1, joined, bias1, h1, acc, moved, pre
 ):
-    rows, channels = cot.shape
-    width = ow.shape[1]
+    rows, width = gg.shape
+    channels = hm.shape[1]
     ext = rows + LAG
     d = dil[1]
     inside = jnp.where(lax.axis_index("seq") == 0, 0.0, 1.0)
 
-    h1[...] = dot(st[...], i3[...], ((1,), (0,)))
-    h1[:LAG, :] = (h1[:LAG, :] + mine[:LAG, :].astype(F32) + other[:LAG, :].astype(F32)) * inside
-    h1[LAG:, :] = h1[LAG:, :] + mine[LAG:, :].astype(F32) + other[LAG:, :].astype(F32)
+    h1[...] = hm[...] + dot(gate_far[...], ow_far[...], ((1,), (0,)))
+    h1[:LAG, :] = h1[:LAG, :] * inside
     near = LAG - pl.multiple_of((d // 8) * 8, 8)
 
     @pl.when(d >= 8)
@@ -135,14 +137,13 @@
     joined[:, channels:] = h1[LAG:, :].astype(BF16)
     for g in range(2):
         pre[:, g * width : (g + 1) * width] = dot(joined[...], w[1, g], ((1,), (0,)))
-    gg[...] = dot(cot[...], ow[1], ((1,), (1,)))
 
     def local(i, total):
         sl = pl.ds(pl.multiple_of(i * 32, 32), 32)
         th, sg = gates(pre[sl, :width] + bias[1, 0:1, :], pre[sl, width:] + bias[1, 1:2, :])
         gate = th * sg
         gate1[sl, :] = gate.astype(BF16)
-        up = gg[sl, :] * scale
+        up = gg[sl, :]
         gf = up * (sg - gate * th)
         gs = up * (gate - gate * sg)
         gl1[sl, :width] = gf.astype(BF16)
@@ -178,9 +179,8 @@
 
 
 def first_back(
-    scale, part, apart, cot, gate0, fa, fb, srow, ow, w, bias1, do1, *refs
+    scale, part, apart, cot, gate0, fa, fb, srow, ow, w, bias1, out, small, adj_s, gl_s, gg
 ):
-    outs, (adj_s, gl_s, out_s, gg) = refs[:-4], refs[-4:]
     rows, channels = cot.shape
     width = ow.shape[1]
     ext = rows + LAG
@@ -203,7 +203,7 @@
     zero = jnp.zeros((8, width), F32)
     tf, ts = lax.fori_loop(0, ext // 64, local, (zero, zero), unroll=2)
     bias = jnp.concatenate([jnp.sum(tf, axis=0, keepdims=True), jnp.sum(ts, axis=0, keepdims=True)], axis=1)
-    out_s[...] = dot(gate0[...], adj_s[...], ((0,), (0,))).reshape(out_s.shape)
+    out[...] = dot(gate0[...], adj_s[...], ((0,), (0,))).astype(BF16)
     r2 = dot(srow[...], gl_s[...], ((1,), (0,)))
     g2 = dot(srow[...], adj_s[...], ((1,), (0,)))
     r = r2[:8] + r2[8:]
@@ -215,23 +215,27 @@
     b_lag = b_lag[:8] + b_lag[8:]
     b_cur = b_cur[:8] + b_cur[8:]
     g = g[DET : 2 * DET] + b_lag[:DET] + b_cur[DET : 2 * DET]
-    small = jnp.concatenate(
+    small[...] = jnp.concatenate(
         [r[: 2 * DET], g, bias, bias1[...], jnp.zeros((5, 2 * width), F32)], axis=0
     )
-    if len(outs) == 2:
-        outs[0][...] = out_s[...].reshape(outs[0].shape)
-        outs[1][...] = small
-    else:
-        m = out_s.shape[1]
-        z = lax.axis_index("seq") >> 1
-        for k in range(4):
-            outs[k][:m, :] = out_s[z ^ k].astype(BF16)
-            outs[k][m : 2 * m, :] = do1[pl.ds(pl.multiple_of((z ^ k) * m, m), m), :]
-            outs[k][2 * m :, :] = small.astype(BF16)
-
-
-def out_grad(scale, gate1, cot, out):
-    out[...] = (dot(gate1[...], cot[...], ((0,), (0,))) * scale).astype(BF16)
+
+
+def pack(out, small, keep, got, *sends):
+    z = lax.axis_index("seq") >> 1
+    m = out.shape[0] // 4
+    h = m // 2
+    for k, send in enumerate(sends):
+        send[:m, :] = out[pl.ds(pl.multiple_of((z ^ k) * m, m), m), :]
+        send[m : m + h, :] = (keep[z ^ k] + got[z ^ k].astype(F32)).astype(BF16)
+        send[m + h :, :] = small[...].astype(BF16)
+
+
+def out_grad(scale, gate1, cot, keep, send, full):
+    x = lax.axis_index("seq") & 1
+    full[...] = (dot(gate1[...], cot[...], ((0,), (0,))) * scale).reshape(full.shape)
+    for z in range(4):
+        keep[z] = full[2 * z + x]
+        send[z] = full[2 * z + 1 - x].astype(BF16)
 
 
 def conv_grad(joined, gl1, keep, send, full):
@@ -261,10 +265,13 @@
 
 
 def half_sum(own, got, blocks, small):
-    m = blocks.shape[0]
-    total = own[...].astype(F32) + got[...].astype(F32)
-    blocks[...] = total[:m].astype(BF16)
-    small[...] = total[m:]
+    x = lax.axis_index("seq") & 1
+    m = blocks.shape[0] // 2
+    h = m // 2
+    blocks[:m, :] = (own[:m, :].astype(F32) + got[:m, :].astype(F32)).astype(BF16)
+    blocks[pl.ds(pl.multiple_of(m + x * h, h), h), :] = own[m : m + h, :]
+    blocks[pl.ds(pl.multiple_of(m + (1 - x) * h, h), h), :] = got[m : m + h, :]
+    small[...] = own[m + h :, :].astype(F32) + got[m + h :, :].astype(F32)
 
 
 def first_conv(iw, small, out):
@@ -354,10 +361,10 @@
     prev = lax.ppermute(strain, "seq", [(i, i + 1) for i in range(n - 1)])
     weight = jnp.transpose(conv_weight, (0, 2, 1, 3))
     full = ext + LAG + MAXSHIFT
-    mine, gate0, fa, fb, st, srow, i3 = pl.pallas_call(
+    ow_far = swap(out_weight[0])
+    gate0, fa, fb, st, srow, i3 = pl.pallas_call(
         first_layer,
         out_shape=[
-            shape((ext, channels), BF16),
             shape((ext, width), BF16),
             shape((ext, width), F32),
             shape((ext, width), F32),
@@ -365,16 +372,19 @@
             shape((16, ext), BF16),
             shape((32, channels), BF16),
         ],
-        in_specs=[SMEM, SMEM] + [VMEM] * 6,
-        out_specs=[VMEM] * 7,
+        in_specs=[SMEM, SMEM] + [VMEM] * 5,
+        out_specs=[VMEM] * 6,
         scratch_shapes=[pltpu.VMEM((8, full), F32), pltpu.VMEM((8, ext), F32)],
         compiler_params=limit(10),
         cost_estimate=cost(2),
         name="first_layer",
-    )(offsets, dilation, prev, strain, input_weight, weight, conv_bias, out_weight)
-    other = swap(mine)
+    )(offsets, dilation, prev, strain, input_weight, weight, conv_bias)
+    gate_far = swap(gate0)
+    hm, gg = call(
+        functools.partial(own_mix, scale), [shape((ext, channels), F32), shape((rows, width), F32)], us=1.5
+    )(st, i3, gate0, out_weight, cotangent)
     part, gl1, gate1, joined, bias1 = pl.pallas_call(
-        functools.partial(second_layer, scale),
+        second_layer,
         out_shape=[
             shape((ext, channels), BF16),
             shape((rows, 2 * width), BF16),
@@ -382,55 +392,53 @@
             shape((rows, 2 * channels), BF16),
             shape((1, 2 * width), F32),
         ],
-        in_specs=[SMEM] + [VMEM] * 8,
+        in_specs=[SMEM] + [VMEM] * 6,
         out_specs=[VMEM] * 5,
         scratch_shapes=[
             pltpu.VMEM((ext, channels), F32),
             pltpu.VMEM((ext, channels), F32),
             pltpu.VMEM((rows + 16, channels), F32),
             pltpu.VMEM((rows, 2 * width), F32),
-            pltpu.VMEM((rows, width), F32),
         ],
         compiler_params=limit(28),
         cost_estimate=cost(7),
         name="second_layer",
-    )(dilation, mine, other, st, i3, weight, conv_bias, out_weight, cotangent)
+    )(dilation, hm, gg, gate_far, ow_far, weight, conv_bias)
     apart = swap(part)
 
     if n == 8:
+        o_keep, o_send = call(
+            functools.partial(out_grad, scale),
+            [shape((4, width // 8, channels), F32), shape((4, width // 8, channels), BF16)],
+            [pltpu.VMEM((8, width // 8, channels), F32)],
+            0.5,
+        )(gate1, cotangent)
+        o_got = along(o_send, 1)
         c_keep, c_send = call(
             conv_grad,
             [shape((4, channels // 4, 2 * width), F32), shape((4, channels // 4, 2 * width), BF16)],
             [pltpu.VMEM((8, channels // 4, 2 * width), F32)],
             1.5,
         )(joined, gl1)
-        c_got = along(c_send, 1)
         apart = after(apart, c_send)
-    do1 = call(functools.partial(out_grad, scale), shape((width, channels), BF16))(gate1, cotangent)
-    m = width // n
-    if n == 8:
-        m = width // 4
-        back_shapes = [shape((2 * m + 16, channels), BF16)] * 4
-        held = (4, m, channels)
-    else:
-        back_shapes = [shape((width, channels), F32), shape((16, 2 * width), F32)]
-        held = (width, channels)
-    back = pl.pallas_call(
+    out0, small = pl.pallas_call(
         functools.partial(first_back, scale),
-        out_shape=back_shapes,
-        in_specs=[VMEM] * 11,
-        out_specs=[VMEM] * len(back_shapes),
+        out_shape=[shape((width, channels), BF16), shape((16, 2 * width), F32)],
+        in_specs=[VMEM] * 10,
+        out_specs=[VMEM] * 2,
         scratch_shapes=[
             pltpu.VMEM((ext, channels), BF16),
             pltpu.VMEM((ext, 2 * width), BF16),
-            pltpu.VMEM(held, F32),
             pltpu.VMEM((ext, width), F32),
         ],
         compiler_params=limit(16),
-        cost_estimate=cost(4),
+        cost_estimate=cost(3),
         name="first_back",
-    )(part, apart, cotangent, gate0, fa, fb, srow, out_weight, weight, bias1, do1)
+    )(part, apart, cotangent, gate0, fa, fb, srow, out_weight, weight, bias1)
     if n == 8:
+        m = width // 4
+        c_got = along(after(c_send, small), 1)
+        back = call(pack, [shape((m + m // 2 + 16, channels), BF16)] * 4, us=0.5)(out0, small, o_keep, o_got)
         got = [along(back[k], 2 * k) for k in (1, 2, 3)]
         c_keep = after(c_keep, back[0])
         c_two, c_send = call(pair_add, pair_shapes(2, channels // 4, 2 * width))(c_keep, c_got)
@@ -445,9 +453,9 @@
         grad_out = call(finish, shape((2, width, channels), F32))(blocks, *got)
     else:
         dw1 = scatter_sum(dot(joined, gl1, ((0,), (0,))), n)
-        do1 = scatter_sum(do1, n)
-        do0 = scatter_sum(back[0], n)
-        small = jnp.sum(gather(back[1], n), axis=0)
+        do1 = scatter_sum(dot(gate1, cotangent, ((0,), (0,))) * scale, n)
+        do0 = scatter_sum(out0, n)
+        small = jnp.sum(gather(small, n), axis=0)
         do = gather(jnp.stack([do0, do1]).astype(BF16), n).astype(F32)
         grad_out = jnp.moveaxis(do, 0, 1).reshape(2, width, channels)
     r, g, bias = small[: 2 * DET], small[2 * DET : 3 * DET], small[3 * DET : 3 * DET + 2]

time: 67.1 us -> 78.6 us (1.17)
  waiting for transfers between devices: 27.2 us -> 36.4 us
  starting transfers between devices: 20.5 us -> 22.8 us
    ppermute x10 -> x11, waiting for transfers between devices: 23.9 us -> 34 us  [along(): return lax.ppermute(x, 'seq', [(i, i ^ k) for i in range(n)])]
    ppermute x10 -> x11, starting transfers between devices: 15.3 us -> 17 us  [along(): return lax.ppermute(x, 'seq', [(i, i ^ k) for i in range(n)])]
    pallas_call x8 -> x10, Pallas kernels: 3.59 us -> 4.8 us  [run(): pl.pallas_call(kernel, out_shape=out_shape, in_specs=[VMEM] * len(args),...]
    pallas_call x3, Pallas kernels: 10.2 us -> 8.98 us  [the longest x1 4.37 us: body(): pl.pallas_call(second_layer, out_shape=[shape((ext, channels), BF16), sha...]
    ppermute x3 -> x4, waiting for transfers between devices: 3.36 us -> 2.41 us  [swap(): return lax.ppermute(x, 'tensor', [(0, 1), (1, 0)])]
  transfers between devices with their start and end apart: 14 -> 16, of which waited for: 8 -> 9; matrix products, arithmetic and copies ran while one was open for 7% -> 4% of each run, Pallas kernels for 8% -> 6%
where the time goes in v4:
time: 78.6 us; the launch traced here: 78.4 us
  waiting for transfers between devices  36.4 us (46%)
  starting transfers between devices  22.8 us (29%)
  Pallas kernels  13.8 us (18%)
  local copies, waits for them, and re-layouts  2.88 us (4%)
  other arithmetic  1.68 us (2%)
  between operations  0.89 us (1%)
    ppermute x11, waiting for transfers between devices, along(): return lax.ppermute(x, 'seq', [(i, i ^ k) for i in range(n)])  34 us
    ppermute x11, starting transfers between devices, along(): return lax.ppermute(x, 'seq', [(i, i ^ k) for i in range(n)])  17 us
    ppermute x1, starting transfers between devices, body(): prev = lax.ppermute(strain, 'seq', [(i, i + 1) for i in range(n - 1)])  5 us
    pallas_call x10, Pallas kernels, run(): pl.pallas_call(kernel, out_shape=out_shape, in_specs=[VMEM] * len(args),...  4.8 us
    pallas_call x1, Pallas kernels, body(): pl.pallas_call(second_layer, out_shape=[shape((ext, channels), BF16), sha...  4.37 us
    pallas_call x1, Pallas kernels, body(): pl.pallas_call(functools.partial(first_back, scale), out_shape=[shape((wi...  2.92 us
    ppermute x4, waiting for transfers between devices, swap(): return lax.ppermute(x, 'tensor', [(0, 1), (1, 0)])  2.41 us
    unnamed x15, local copies, waits for them, and re-layouts  1.9 us
  transfers between devices with their start and end apart: 16, of which 9 were waited for; matrix products, arithmetic and copies ran while one was open for 4% of the time, Pallas kernels for 6%

profile of v4, /device:TPU:0, one launch (start us, length us, event | category | flops | bytes accessed | tf_op | source)
XLA Modules:
  0.0 78.4 jit_solution(13154858283946700479)
XLA Ops:
  0.6 0.0 copy-start.2
  0.6 0.0 copy-start.4
  0.7 0.0 copy-start.3
  0.7 0.0 copy-start.6
  0.7 0.0 copy-start.5
  0.7 5.0 %collective-permute-start = (f32[3,896]{1,0:T(4,128)}, f32[3,896]{1,0:T(4,128)S(1)}, u32[]{:S(2)}, u32[]{:S(2)}) collective-permute-start(f32[3,896]{1,0:T(4,128)} %own.1), channel_id=1, source_target_pairs={{0,2},{2,4},{4,6},{6,8},{8,10},{10,12},{12,14},{1,3},{3,5},{5,7},{... | collective-permute-start | bytes 32264 | tf_op jit(solution)/shard_map/ppermute | solution.py:361
  5.7 1.9 %copy.14 = bf16[2,1024,2,256]{3,1,2,0:T(8,128)(2,1)S(1)} copy(bf16[2,1024,2,256]{3,2,1,0:T(2,128)(2,1)} %param.12) | data formatting | bytes 4194304 | tf_op args[4]
  7.6 0.0 collective-permute-done.prev
  7.6 0.0 copy-done.2
  7.6 0.0 copy-done.4
  7.6 0.0 copy-done.3
  7.6 0.0 copy-done.6
  7.6 0.0 copy-done.5
  7.6 0.0 copy-start
  7.6 0.0 copy-start.1
  7.6 1.7 %first_layer.1 = (bf16[1408,256]{1,0:T(8,128)(2,1)S(1)}, f32[1408,256]{1,0:T(8,128)S(1)}, f32[1408,256]{1,0:T(8,128)S(1)}, bf16[1408,32]{1,0:T(8,128)(2,1)S(1)},...) custom-call(s32[3]{0:T(128)S(1)} %copy-done.5, s32[2]{0:T(128)S(1)} %copy-done.6, ...), custom_call_target="tpu_custom_call" | custom-call | flops 1600000000 | bytes 6000000 | tf_op jit(solution)/shard_map/first_layer/pallas_call | solution.py:365
  9.3 0.1 collective-permute-start.1
  9.4 0.0 copy-done
  9.5 0.5 collective-permute-start.2
  10.0 0.0 copy-done.1
  10.0 1.2 %own_mix.1 = (f32[1408,512]{1,0:T(8,128)S(1)}, f32[896,256]{1,0:T(8,128)S(1)}) custom-call(bf16[1408,32]{1,0:T(8,128)(2,1)S(1)} %get-tuple-element.36.st, bf16[32,512]{1,0:T(8,128)(2,1)S(1)} %get-tuple-element.37.i3, bf16[1408,256]{1,0:T(8,128)(2,1)S(1)} %get-tuple-element.38.gate0, bf16[2,256,512]{2,1,0:T(8,128)(2,1)S(1)} %copy-done, ...), custom_call_target="tpu_custom_call" | custom-call | flops 1200000000 | bytes 4500000 | tf_op jit(solution)/shard_map/own_mix/pallas_call | solution.py:339
  11.2 0.8 %collective-permute-done.2.ow_far = bf16[256,512]{1,0:T(8,128)(2,1)S(1)} collective-permute-done((bf16[256,512]{1,0:T(8,128)(2,1)S(1)}, bf16[256,512]{1,0:T(8,128)(2,1)S(1)}, u32[]{:S(2)}, u32[]{:S(2)}) %collective-permute-start.2) | collective-permute-done | bytes 262176 | tf_op jit(solution)/shard_map/ppermute | solution.py:26
  12.0 0.0 collective-permute-done.1.gate_far
  12.0 4.4 %second_layer.1 = (bf16[1408,512]{1,0:T(8,128)(2,1)S(1)}, bf16[896,512]{1,0:T(8,128)(2,1)S(1)}, bf16[896,256]{1,0:T(8,128)(2,1)S(1)}, bf16[896,1024]{1,0:T(8,128)(2,1)S(1)}, f32[1,512]{1,0:T(1,128)S(1)}) custom-call(s32[2]{0:T(128)S(1)} %copy-done.6, f32[1408,512]{1,0:T(8,128)S(1)} %get-tuple-element.39.hm, f32[896,256]{1,0:T(8,128)S(1)} %get-tuple-element.40.gg, ...), custom_call_target="tpu_custom_call" | custom-call | flops 5600000000 | bytes 21000000 | tf_op jit(solution)/shard_map/second_layer/pallas_call | solution.py:386
  16.4 0.2 collective-permute-start.3
  16.6 1.5 %conv_grad.1 = (f32[4,128,512]{2,1,0:T(8,128)S(1)}, bf16[4,128,512]{2,1,0:T(8,128)(2,1)S(1)}) custom-call(bf16[896,1024]{1,0:T(8,128)(2,1)S(1)} %get-tuple-element.42.joined, bf16[896,512]{1,0:T(8,128)(2,1)S(1)} %get-tuple-element.43.gl1), custom_call_target="tpu_custom_call" | custom-call | flops 1200000000 | bytes 4500000 | tf_op jit(solution)/shard_map/conv_grad/pallas_call | solution.py:339
  18.0 1.6 %collective-permute-done.3.apart = bf16[1408,512]{1,0:T(8,128)(2,1)S(1)} collective-permute-done((bf16[1408,512]{1,0:T(8,128)(2,1)S(1)}, bf16[1408,512]{1,0:T(8,128)(2,1)S(1)}, u32[]{:S(2)}, u32[]{:S(2)}) %collective-permute-start.3) | collective-permute-done | bytes 1441824 | tf_op jit(solution)/shard_map/ppermute | solution.py:26
  19.6 2.9 %first_back.1 = (bf16[256,512]{1,0:T(8,128)(2,1)S(1)}, f32[16,512]{1,0:T(8,128)S(1)}) custom-call(bf16[1408,512]{1,0:T(8,128)(2,1)S(1)} %get-tuple-element.41.part, bf16[1408,512]{1,0:T(8,128)(2,1)S(1)} %collective-permute-done.3.apart, bf16[896,512]{1,0:T(8,128)(2,1)S(1)} %copy-done.1, bf16[1408,256]{1,0:T(8,128)(2,1)S(1)} %get-tuple-element.38.gate0, ...), custom_call_target="tpu_custom_call" | custom-call | flops 2400000000 | bytes 9000000 | tf_op jit(solution)/shard_map/first_back/pallas_call | solution.py:424
  22.6 2.0 %collective-permute-start.10 = (bf16[4,128,512]{2,1,0:T(8,128)(2,1)S(1)}, bf16[4,128,512]{2,1,0:T(8,128)(2,1)S(1)}, u32[]{:S(2)}, u32[]{:S(2)}) collective-permute-start(bf16[4,128,512]{2,1,0:T(8,128)(2,1)S(1)} %get-tuple-element.62), channel_id=1, source_target_pairs={{0,2},{2,0},{4,6},{6,4},{8,10},{10,8},{12,14},{14,12},{1,3},{3,1},... | collective-permute-start | bytes 1572872 | tf_op jit(solution)/shard_map/ppermute | solution.py:308
  24.6 0.5 out_grad.1
  25.1 0.1 collective-permute-start.4
  25.2 14.4 %collective-permute-done.4.got = bf16[4,32,512]{2,1,0:T(8,128)(2,1)S(1)} collective-permute-done((bf16[4,32,512]{2,1,0:T(8,128)(2,1)S(1)}, bf16[4,32,512]{2,1,0:T(8,128)(2,1)S(1)}, u32[]{:S(2)}, u32[]{:S(2)}) %collective-permute-start.4) | collective-permute-done | bytes 131104 | tf_op jit(solution)/shard_map/ppermute | solution.py:308
  39.7 2.8 %collective-permute-start.5 = (bf16[112,512]{1,0:T(8,128)(2,1)S(1)}, bf16[112,512]{1,0:T(8,128)(2,1)S(1)}, u32[]{:S(2)}, u32[]{:S(2)}) collective-permute-start(bf16[112,512]{1,0:T(8,128)(2,1)S(1)} %get-tuple-element.56), channel_id=1, source_target_pairs={{0,4},{2,6},{4,0},{6,2},{8,12},{10,14},{12,8},{14,10},{1,5},{3,7},... | collective-permute-start | bytes 344072 | tf_op jit(solution)/shard_map/ppermute | solution.py:308
  42.5 2.6 %collective-permute-start.6 = (bf16[112,512]{1,0:T(8,128)(2,1)S(1)}, bf16[112,512]{1,0:T(8,128)(2,1)S(1)}, u32[]{:S(2)}, u32[]{:S(2)}) collective-permute-start(bf16[112,512]{1,0:T(8,128)(2,1)S(1)} %get-tuple-element.57), channel_id=1, source_target_pairs={{0,8},{2,10},{4,12},{6,14},{8,0},{10,2},{12,4},{14,6},{1,9},{3,11}... | collective-permute-start | bytes 344072 | tf_op jit(solution)/shard_map/ppermute | solution.py:308
  45.1 0.0 collective-permute-start.7
  45.1 1.3 %collective-permute-done.5.r1 = bf16[112,512]{1,0:T(8,128)(2,1)S(1)} collective-permute-done((bf16[112,512]{1,0:T(8,128)(2,1)S(1)}, bf16[112,512]{1,0:T(8,128)(2,1)S(1)}, u32[]{:S(2)}, u32[]{:S(2)}) %collective-permute-start.5) | collective-permute-done | bytes 114720 | tf_op jit(solution)/shard_map/ppermute | solution.py:308
  46.3 7.3 %collective-permute-done.6.r2 = bf16[112,512]{1,0:T(8,128)(2,1)S(1)} collective-permute-done((bf16[112,512]{1,0:T(8,128)(2,1)S(1)}, bf16[112,512]{1,0:T(8,128)(2,1)S(1)}, u32[]{:S(2)}, u32[]{:S(2)}) %collective-permute-start.6) | collective-permute-done | bytes 114720 | tf_op jit(solution)/shard_map/ppermute | solution.py:308
  53.6 0.0 collective-permute-done.7.r3
  53.6 0.1 quarter_sum.1.own
  53.8 0.7 collective-permute-start.8
  54.4 0.0 collective-permute-done.10.got
  54.4 0.1 pair_add.1
  54.5 1.9 %collective-permute-start.11 = (bf16[2,128,512]{2,1,0:T(8,128)(2,1)S(1)}, bf16[2,128,512]{2,1,0:T(8,128)(2,1)S(1)}, u32[]{:S(2)}, u32[]{:S(2)}) collective-permute-start(bf16[2,128,512]{2,1,0:T(8,128)(2,1)S(1)} %get-tuple-element.64), channel_id=1, source_target_pairs={{0,4},{2,6},{4,0},{6,2},{8,12},{10,14},{12,8},{14,10},{1,5},{3,7},... | collective-permute-start | bytes 786440 | tf_op jit(solution)/shard_map/ppermute | solution.py:308
  56.4 2.2 %collective-permute-done.8.got = bf16[112,512]{1,0:T(8,128)(2,1)S(1)} collective-permute-done((bf16[112,512]{1,0:T(8,128)(2,1)S(1)}, bf16[112,512]{1,0:T(8,128)(2,1)S(1)}, u32[]{:S(2)}, u32[]{:S(2)}) %collective-permute-start.8) | collective-permute-done | bytes 114720 | tf_op jit(solution)/shard_map/ppermute | solution.py:308
  58.7 2.5 %collective-permute-start.15 = (bf16[128,512]{1,0:T(8,128)(2,1)S(1)}, bf16[128,512]{1,0:T(8,128)(2,1)S(1)}, u32[]{:S(2)}, u32[]{:S(2)}) collective-permute-start(bf16[128,512]{1,0:T(8,128)(2,1)S(1)} %get-tuple-element.67.own), channel_id=1, source_target_pairs={{0,12},{2,14},{4,8},{6,10},{8,4},{10,6},{12,0},{14,2},{1,13},{3,15... | collective-permute-start | bytes 393224 | tf_op jit(solution)/shard_map/ppermute | solution.py:308
  61.2 0.8 %collective-permute-start.14 = (bf16[128,512]{1,0:T(8,128)(2,1)S(1)}, bf16[128,512]{1,0:T(8,128)(2,1)S(1)}, u32[]{:S(2)}, u32[]{:S(2)}) collective-permute-start(bf16[128,512]{1,0:T(8,128)(2,1)S(1)} %get-tuple-element.67.own), channel_id=1, source_target_pairs={{0,8},{2,10},{4,12},{6,14},{8,0},{10,2},{12,4},{14,6},{1,9},{3,11}... | collective-permute-start | bytes 393224 | tf_op jit(solution)/shard_map/ppermute | solution.py:308
  62.0 1.1 %collective-permute-start.13 = (bf16[128,512]{1,0:T(8,128)(2,1)S(1)}, bf16[128,512]{1,0:T(8,128)(2,1)S(1)}, u32[]{:S(2)}, u32[]{:S(2)}) collective-permute-start(bf16[128,512]{1,0:T(8,128)(2,1)S(1)} %get-tuple-element.67.own), channel_id=1, source_target_pairs={{0,4},{2,6},{4,0},{6,2},{8,12},{10,14},{12,8},{14,10},{1,5},{3,7},... | collective-permute-start | bytes 393224 | tf_op jit(solution)/shard_map/ppermute | solution.py:308
  63.1 0.6 reshape.16
  63.7 0.0 collective-permute-start.9
  63.7 0.2 first_conv.1
  64.0 0.2 stack.9
  64.1 0.0 collective-permute-done.11.got
  64.1 0.1 pair_add_again.1
  64.2 2.5 %collective-permute-start.12 = (bf16[128,512]{1,0:T(8,128)(2,1)S(1)}, bf16[128,512]{1,0:T(8,128)(2,1)S(1)}, u32[]{:S(2)}, u32[]{:S(2)}) collective-permute-start(bf16[128,512]{1,0:T(8,128)(2,1)S(1)} %get-tuple-element.66), channel_id=1, source_target_pairs={{0,8},{2,10},{4,12},{6,14},{8,0},{10,2},{12,4},{14,6},{1,9},{3,11}... | collective-permute-start | bytes 393224 | tf_op jit(solution)/shard_map/ppermute | solution.py:308
  66.7 0.0 collective-permute-done.9
  66.7 0.6 slice_add_fusion
  67.3 1.5 %collective-permute-done.15.r3 = bf16[128,512]{1,0:T(8,128)(2,1)S(1)} collective-permute-done((bf16[128,512]{1,0:T(8,128)(2,1)S(1)}, bf16[128,512]{1,0:T(8,128)(2,1)S(1)}, u32[]{:S(2)}, u32[]{:S(2)}) %collective-permute-start.15) | collective-permute-done | bytes 131104 | tf_op jit(solution)/shard_map/ppermute | solution.py:308
  68.8 6.9 %collective-permute-done.14.r2 = bf16[128,512]{1,0:T(8,128)(2,1)S(1)} collective-permute-done((bf16[128,512]{1,0:T(8,128)(2,1)S(1)}, bf16[128,512]{1,0:T(8,128)(2,1)S(1)}, u32[]{:S(2)}, u32[]{:S(2)}) %collective-permute-start.14) | collective-permute-done | bytes 131104 | tf_op jit(solution)/shard_map/ppermute | solution.py:308
  75.8 0.0 collective-permute-done.13.r1
  75.8 1.0 %finish.1 = f32[2,256,512]{2,1,0:T(8,128)} custom-call(bf16[128,512]{1,0:T(8,128)(2,1)S(1)} %get-tuple-element.67.own, bf16[128,512]{1,0:T(8,128)(2,1)S(1)} %collective-permute-done.13.r1, bf16[128,512]{1,0:T(8,128)(2,1)S(1)} %collective-permute-done.14.r2, bf16[128,512]{1,0:T(8,128)(2,1)S(1)} %collective-permute-done.15.r3), custom_call_target="tpu_custom_call" | custom-call | flops 800000000 | bytes 3000000 | tf_op jit(solution)/shard_map/finish/pallas_call | solution.py:339
  76.8 0.4 collective-permute-done.12
  77.2 0.2 stack.10
  77.4 1.0 %pad_maximum_fusion = f32[2,128,2,256]{3,2,1,0:T(2,128)} fusion(f32[1,128,2,256]{3,2,1,0:T(2,128)S(1)} %stack.10, f32[1,128,2,256]{3,2,1,0:T(2,128)S(1)} %stack.9), kind=kLoop, calls=%fused_computation.1 | loop fusion | flops 131072 | bytes 1048576 | tf_op jit(solution)/shard_map/stack | solution.py:471
  (6 shorter events, 0.1 us)
Async XLA Ops:
  0.6 6.9 %copy-start.2 = (f32[3,896]{1,0:T(4,128)S(1)}, f32[3,896]{1,0:T(4,128)}, u32[]{:S(2)}) copy-start(f32[3,896]{1,0:T(4,128)} %own.1) | copy-start | bytes 32260
  0.6 6.9 %copy-start.4 = (f32[2,2,256]{2,1,0:T(2,128)S(1)}, f32[2,2,256]{2,1,0:T(2,128)}, u32[]{:S(2)}) copy-start(f32[2,2,256]{2,1,0:T(2,128)} %bias.3) | copy-start | bytes 12292
  0.7 6.9 %copy-start.3 = (f32[3,512]{1,0:T(4,128)S(1)}, f32[3,512]{1,0:T(4,128)}, u32[]{:S(2)}) copy-start(f32[3,512]{1,0:T(4,128)} %iw.3) | copy-start | bytes 18436
  0.7 6.9 %copy-start.6 = (s32[2]{0:T(128)S(1)}, s32[2]{0:T(128)}, u32[]{:S(2)}) copy-start(s32[2]{0:T(128)} %dil.3) | copy-start | bytes 28
  0.7 6.9 %copy-start.5 = (s32[3]{0:T(128)S(1)}, s32[3]{0:T(128)}, u32[]{:S(2)}) copy-start(s32[3]{0:T(128)} %offs.1) | copy-start | bytes 40
  0.7 6.9 %collective-permute-start = (f32[3,896]{1,0:T(4,128)}, f32[3,896]{1,0:T(4,128)S(1)}, u32[]{:S(2)}, u32[]{:S(2)}) collective-permute-start(f32[3,896]{1,0:T(4,128)} %own.1), channel_id=1, source_target_pairs={{0,2},{2,4},{4,6},{6,8},{8,10},{10,12},{12,14},{1,3},{3,5},{5,7},{... | collective-permute-start | bytes 32264 | tf_op jit(solution)/shard_map/ppermute | solution.py:361
  7.6 1.8 %copy-start = (bf16[2,256,512]{2,1,0:T(8,128)(2,1)S(1)}, bf16[2,256,512]{2,1,0:T(8,128)(2,1)}, u32[]{:S(2)}) copy-start(bf16[2,256,512]{2,1,0:T(8,128)(2,1)} %ow.3) | copy-start | bytes 1572868
  7.6 2.4 %copy-start.1 = (bf16[896,512]{1,0:T(8,128)(2,1)S(1)}, bf16[896,512]{1,0:T(8,128)(2,1)}, u32[]{:S(2)}) copy-start(bf16[896,512]{1,0:T(8,128)(2,1)} %cot.5) | copy-start | bytes 2752516
  9.3 2.6 %collective-permute-start.1 = (bf16[1408,256]{1,0:T(8,128)(2,1)S(1)}, bf16[1408,256]{1,0:T(8,128)(2,1)S(1)}, u32[]{:S(2)}, u32[]{:S(2)}) collective-permute-start(bf16[1408,256]{1,0:T(8,128)(2,1)S(1)} %get-tuple-element.38.gate0), channel_id=1, source_target_pairs={{0,1},{1,0},{2,3},{3,2},{4,5},{5,4},{6,7},{7,6},{8,9},{9,8},{10,11... | collective-permute-start | bytes 2162696 | tf_op jit(solution)/shard_map/ppermute | solution.py:26
  9.5 2.5 %collective-permute-start.2 = (bf16[256,512]{1,0:T(8,128)(2,1)S(1)}, bf16[256,512]{1,0:T(8,128)(2,1)S(1)}, u32[]{:S(2)}, u32[]{:S(2)}) collective-permute-start(bf16[256,512]{1,0:T(8,128)(2,1)S(1)} %slice_bitcast_fusion), channel_id=1, source_target_pairs={{0,1},{1,0},{2,3},{3,2},{4,5},{5,4},{6,7},{7,6},{8,9},{9,8},{10,11... | collective-permute-start | bytes 786440 | tf_op jit(solution)/shard_map/ppermute | solution.py:26
  16.4 3.3 %collective-permute-start.3 = (bf16[1408,512]{1,0:T(8,128)(2,1)S(1)}, bf16[1408,512]{1,0:T(8,128)(2,1)S(1)}, u32[]{:S(2)}, u32[]{:S(2)}) collective-permute-start(bf16[1408,512]{1,0:T(8,128)(2,1)S(1)} %get-tuple-element.41.part), channel_id=1, source_target_pairs={{0,1},{1,0},{2,3},{3,2},{4,5},{5,4},{6,7},{7,6},{8,9},{9,8},{10,11... | collective-permute-start | bytes 4325384 | tf_op jit(solution)/shard_map/ppermute | solution.py:26
  22.6 31.9 %collective-permute-start.10 = (bf16[4,128,512]{2,1,0:T(8,128)(2,1)S(1)}, bf16[4,128,512]{2,1,0:T(8,128)(2,1)S(1)}, u32[]{:S(2)}, u32[]{:S(2)}) collective-permute-start(bf16[4,128,512]{2,1,0:T(8,128)(2,1)S(1)} %get-tuple-element.62), channel_id=1, source_target_pairs={{0,2},{2,0},{4,6},{6,4},{8,10},{10,8},{12,14},{14,12},{1,3},{3,1},... | collective-permute-start | bytes 1572872 | tf_op jit(solution)/shard_map/ppermute | solution.py:308
  25.1 14.5 %collective-permute-start.4 = (bf16[4,32,512]{2,1,0:T(8,128)(2,1)S(1)}, bf16[4,32,512]{2,1,0:T(8,128)(2,1)S(1)}, u32[]{:S(2)}, u32[]{:S(2)}) collective-permute-start(bf16[4,32,512]{2,1,0:T(8,128)(2,1)S(1)} %get-tuple-element.54), channel_id=1, source_target_pairs={{0,2},{2,0},{4,6},{6,4},{8,10},{10,8},{12,14},{14,12},{1,3},{3,1},... | collective-permute-start | bytes 393224 | tf_op jit(solution)/shard_map/ppermute | solution.py:308
  39.7 6.7 %collective-permute-start.5 = (bf16[112,512]{1,0:T(8,128)(2,1)S(1)}, bf16[112,512]{1,0:T(8,128)(2,1)S(1)}, u32[]{:S(2)}, u32[]{:S(2)}) collective-permute-start(bf16[112,512]{1,0:T(8,128)(2,1)S(1)} %get-tuple-element.56), channel_id=1, source_target_pairs={{0,4},{2,6},{4,0},{6,2},{8,12},{10,14},{12,8},{14,10},{1,5},{3,7},... | collective-permute-start | bytes 344072 | tf_op jit(solution)/shard_map/ppermute | solution.py:308
  42.5 11.1 %collective-permute-start.6 = (bf16[112,512]{1,0:T(8,128)(2,1)S(1)}, bf16[112,512]{1,0:T(8,128)(2,1)S(1)}, u32[]{:S(2)}, u32[]{:S(2)}) collective-permute-start(bf16[112,512]{1,0:T(8,128)(2,1)S(1)} %get-tuple-element.57), channel_id=1, source_target_pairs={{0,8},{2,10},{4,12},{6,14},{8,0},{10,2},{12,4},{14,6},{1,9},{3,11}... | collective-permute-start | bytes 344072 | tf_op jit(solution)/shard_map/ppermute | solution.py:308
  45.1 8.6 %collective-permute-start.7 = (bf16[112,512]{1,0:T(8,128)(2,1)S(1)}, bf16[112,512]{1,0:T(8,128)(2,1)S(1)}, u32[]{:S(2)}, u32[]{:S(2)}) collective-permute-start(bf16[112,512]{1,0:T(8,128)(2,1)S(1)} %get-tuple-element.58), channel_id=1, source_target_pairs={{0,12},{2,14},{4,8},{6,10},{8,4},{10,6},{12,0},{14,2},{1,13},{3,15... | collective-permute-start | bytes 344072 | tf_op jit(solution)/shard_map/ppermute | solution.py:308
  53.8 4.9 %collective-permute-start.8 = (bf16[112,512]{1,0:T(8,128)(2,1)S(1)}, bf16[112,512]{1,0:T(8,128)(2,1)S(1)}, u32[]{:S(2)}, u32[]{:S(2)}) collective-permute-start(bf16[112,512]{1,0:T(8,128)(2,1)S(1)} %quarter_sum.1.own), channel_id=1, source_target_pairs={{0,2},{2,0},{4,6},{6,4},{8,10},{10,8},{12,14},{14,12},{1,3},{3,1},... | collective-permute-start | bytes 344072 | tf_op jit(solution)/shard_map/ppermute | solution.py:308
  54.5 9.6 %collective-permute-start.11 = (bf16[2,128,512]{2,1,0:T(8,128)(2,1)S(1)}, bf16[2,128,512]{2,1,0:T(8,128)(2,1)S(1)}, u32[]{:S(2)}, u32[]{:S(2)}) collective-permute-start(bf16[2,128,512]{2,1,0:T(8,128)(2,1)S(1)} %get-tuple-element.64), channel_id=1, source_target_pairs={{0,4},{2,6},{4,0},{6,2},{8,12},{10,14},{12,8},{14,10},{1,5},{3,7},... | collective-permute-start | bytes 786440 | tf_op jit(solution)/shard_map/ppermute | solution.py:308
  58.7 10.2 %collective-permute-start.15 = (bf16[128,512]{1,0:T(8,128)(2,1)S(1)}, bf16[128,512]{1,0:T(8,128)(2,1)S(1)}, u32[]{:S(2)}, u32[]{:S(2)}) collective-permute-start(bf16[128,512]{1,0:T(8,128)(2,1)S(1)} %get-tuple-element.67.own), channel_id=1, source_target_pairs={{0,12},{2,14},{4,8},{6,10},{8,4},{10,6},{12,0},{14,2},{1,13},{3,15... | collective-permute-start | bytes 393224 | tf_op jit(solution)/shard_map/ppermute | solution.py:308
  61.2 14.6 %collective-permute-start.14 = (bf16[128,512]{1,0:T(8,128)(2,1)S(1)}, bf16[128,512]{1,0:T(8,128)(2,1)S(1)}, u32[]{:S(2)}, u32[]{:S(2)}) collective-permute-start(bf16[128,512]{1,0:T(8,128)(2,1)S(1)} %get-tuple-element.67.own), channel_id=1, source_target_pairs={{0,8},{2,10},{4,12},{6,14},{8,0},{10,2},{12,4},{14,6},{1,9},{3,11}... | collective-permute-start | bytes 393224 | tf_op jit(solution)/shard_map/ppermute | solution.py:308
  62.0 13.8 %collective-permute-start.13 = (bf16[128,512]{1,0:T(8,128)(2,1)S(1)}, bf16[128,512]{1,0:T(8,128)(2,1)S(1)}, u32[]{:S(2)}, u32[]{:S(2)}) collective-permute-start(bf16[128,512]{1,0:T(8,128)(2,1)S(1)} %get-tuple-element.67.own), channel_id=1, source_target_pairs={{0,4},{2,6},{4,0},{6,2},{8,12},{10,14},{12,8},{14,10},{1,5},{3,7},... | collective-permute-start | bytes 393224 | tf_op jit(solution)/shard_map/ppermute | solution.py:308
  63.7 3.0 %collective-permute-start.9 = (f32[3,512]{1,0:T(4,128)S(1)}, f32[3,512]{1,0:T(4,128)S(1)}, u32[]{:S(2)}, u32[]{:S(2)}) collective-permute-start(f32[3,512]{1,0:T(4,128)S(1)} %slice.10), channel_id=1, source_target_pairs={{0,1},{1,0},{2,3},{3,2},{4,5},{5,4},{6,7},{7,6},{8,9},{9,8},{10,11... | collective-permute-start | bytes 18440 | tf_op jit(solution)/shard_map/ppermute | solution.py:26
  64.2 12.9 %collective-permute-start.12 = (bf16[128,512]{1,0:T(8,128)(2,1)S(1)}, bf16[128,512]{1,0:T(8,128)(2,1)S(1)}, u32[]{:S(2)}, u32[]{:S(2)}) collective-permute-start(bf16[128,512]{1,0:T(8,128)(2,1)S(1)} %get-tuple-element.66), channel_id=1, source_target_pairs={{0,8},{2,10},{4,12},{6,14},{8,0},{10,2},{12,4},{14,6},{1,9},{3,11}... | collective-permute-start | bytes 393224 | tf_op jit(solution)/shard_map/ppermute | solution.py:308
